TPU v7x, 512 devices: a whole 4x4x16 slice. The times are simulated.
512 devices in a mesh: ctx: 64 (over z, y), vid: 8 (over x, core).
Axes of the slice: x: 4, y: 4, z: 16, core: 2. Of those that a mesh axis runs over, the one named last changes fastest.
Arguments:
- features: bfloat16 [8, 128, 8, 32, 256], P('vid', 'ctx'), may hold values from -6 to 6
- grad_out: bfloat16 [8, 128, 8, 32, 128], P('vid', 'ctx'), may hold values from -6 to 6
- mean_saved: float32 [8, 32], P('vid'), may hold values from -3 to 3
- rstd_saved: float32 [8, 32], P('vid'), may hold values from 0.5 to 2
- latent: float32 [8, 32, 16, 16], P('vid'), may hold values from -6 to 6
- gamma: float32 [256], replicated, may hold values from 0.5 to 1.5
- beta: float32 [256], replicated, may hold values from -3 to 3
- w_scale: float32 [16, 256], replicated, may hold values from -1.5 to 1.5
- b_scale: float32 [256], replicated, may hold values from -3 to 3
- w_shift: float32 [16, 256], replicated, may hold values from -1.5 to 1.5
- b_shift: float32 [256], replicated, may hold values from -3 to 3
- kernel: bfloat16 [6912, 128], replicated, may hold values from -0.078125 to 0.078125
Outputs:
- features_grad: bfloat16 [8, 128, 8, 32, 256], P('vid', 'ctx')
- kernel_grad: float32 [6912, 128], P('ctx', 'vid')
- mod_grads: float32 [2, 16, 256], replicated
- vector_grads: float32 [4, 256], replicated
- latent_grad: float32 [8, 64, 16, 8], P('vid', 'ctx')
All inputs are finite; a program needn't handle non-finite values.
Results may differ from a plain program's by a relative error of at most 0.0029.
Values may be sent and summed in bfloat16 or wider, within the bound.
A program may use at most 64 MiB of HBM per device.

v0:
```python
import jax
import jax.numpy as jnp
from jax import lax
from jax.sharding import PartitionSpec as P

FR_DEV = 2
H = 8
W = 32
C = 256
CO = 128
G = 32
LP = 16


highest = lax.Precision.HIGHEST


def passed_along(value, axis, steps):
    count = lax.axis_size(axis)
    leading, last = (max(0, -steps), min(count, count - steps))
    return lax.ppermute(value, axis, [(source, source + steps) for source in range(leading, last)])


def swapped(value, axis, apart):
    mask = 2**apart
    pairs = [(source, source ^ mask) for source in range(lax.axis_size(axis))]
    return lax.ppermute(value, axis, pairs)


def spread_frame(table):
    grid = table.reshape(H // 4, W // 4, C)
    wide = jnp.broadcast_to(grid[:, None, :, None, :], (H // 4, 4, W // 4, 4, C))
    return wide.reshape(1, H, W, C)


def pool_frames(field):
    frames = field.shape[0]
    return field.reshape(frames, H // 4, 4, W // 4, 4, C).sum(axis=(0, 2, 4)).reshape(LP, C)


def transpose_conv(grad_pad, tap_weights, frames):
    total = jnp.zeros((frames * H * W, C), jnp.float32)
    for frame_tap in range(3):
        for row_tap in range(3):
            for col_tap in range(3):
                source = grad_pad[
                    2 - frame_tap : 2 - frame_tap + frames,
                    2 - row_tap : 2 - row_tap + H,
                    2 - col_tap : 2 - col_tap + W,
                ].reshape(frames * H * W, CO)
                total = total + lax.dot_general(
                    source,
                    tap_weights[frame_tap, row_tap, col_tap],
                    (((1,), (1,)), ((), ())),
                    preferred_element_type=jnp.float32,
                )
    return total.reshape(frames, H, W, C)


def local(
    features,
    grad_out,
    mean_saved,
    rstd_saved,
    latent,
    gamma,
    beta,
    w_scale,
    b_scale,
    w_shift,
    b_shift,
    kernel,
):
    device = lax.axis_index("ctx")
    frames_in = features[0]
    grads_in = grad_out[0]
    mean_chan = jnp.broadcast_to(mean_saved[0][:, None], (G, C // G)).reshape(C)
    rstd_chan = jnp.broadcast_to(rstd_saved[0][:, None], (G, C // G)).reshape(C)
    normed = (frames_in.astype(jnp.float32) - mean_chan) * rstd_chan
    latent_frame = lax.dynamic_index_in_dim(latent[0], device // 2, 0, keepdims=False)
    scale_tab = jnp.einsum("zp,zc->pc", latent_frame, w_scale, precision=highest) + b_scale
    shift_tab = jnp.einsum("zp,zc->pc", latent_frame, w_shift, precision=highest) + b_shift
    scale_map = spread_frame(scale_tab)
    shift_map = spread_frame(shift_tab)
    base_map = normed * gamma + beta
    modulated = base_map * scale_map + shift_map
    squashed = jax.nn.sigmoid(modulated)
    activated = (modulated * squashed).astype(jnp.bfloat16)
    before = passed_along(activated, "ctx", 1)
    leading = jnp.broadcast_to(activated[:1], before.shape)
    before = jnp.where(device == 0, leading, before)
    padded = jnp.pad(jnp.concatenate([before, activated], 0), ((0, 0), (1, 1), (1, 1), (0, 0)))
    tap_weights = kernel.reshape(3, 3, 3, C, CO)
    grads_rows = grads_in.reshape(FR_DEV * H * W, CO)
    pieces = []
    for frame_tap in range(3):
        for row_tap in range(3):
            for col_tap in range(3):
                window = padded[
                    frame_tap : frame_tap + FR_DEV, row_tap : row_tap + H, col_tap : col_tap + W
                ].reshape(FR_DEV * H * W, C)
                pieces.append(
                    lax.dot_general(
                        window,
                        grads_rows,
                        (((0,), (0,)), ((), ())),
                        preferred_element_type=jnp.float32,
                    )
                )
    kernel_term = jnp.stack(pieces).reshape(27 * C, CO)
    beyond = passed_along(grads_in, "ctx", -1)
    grad_pad = jnp.pad(jnp.concatenate([grads_in, beyond], 0), ((2, 0), (1, 1), (1, 1), (0, 0)))
    extended = transpose_conv(grad_pad, tap_weights, FR_DEV + 2)
    act_grad = extended[2:]
    virtual = jnp.where(device == 0, extended[0] + extended[1], 0.0)
    act_grad = act_grad.at[0].add(virtual)
    pre_grad = act_grad * squashed * (1.0 + modulated * (1.0 - squashed))
    features_grad = (pre_grad * scale_map * gamma * rstd_chan).astype(jnp.bfloat16)
    scale_pool = pool_frames(pre_grad * base_map)
    shift_pool = pool_frames(pre_grad)
    mod_part = jnp.stack(
        [
            jnp.einsum("zp,pc->zc", latent_frame, scale_pool, precision=highest),
            jnp.einsum("zp,pc->zc", latent_frame, shift_pool, precision=highest),
        ]
    )
    vec_part = jnp.stack(
        [
            jnp.sum(pre_grad * scale_map * normed, axis=(0, 1, 2)),
            jnp.sum(pre_grad * scale_map, axis=(0, 1, 2)),
            jnp.sum(scale_pool, axis=0),
            jnp.sum(shift_pool, axis=0),
        ]
    )
    latent_sum = jnp.einsum("zc,pc->zp", w_scale, scale_pool, precision=highest) + jnp.einsum(
        "zc,pc->zp", w_shift, shift_pool, precision=highest
    )
    half_len = LP // 2
    parity = device % 2
    own_half = lax.dynamic_slice_in_dim(latent_sum, parity * half_len, half_len, 1)
    far_half = lax.dynamic_slice_in_dim(latent_sum, (1 - parity) * half_len, half_len, 1)
    received = swapped(far_half, "ctx", 0)
    latent_grad = (own_half + received)[None, None]
    mod_grads, vector_grads = lax.psum((mod_part, vec_part), ("ctx", "vid"))
    kernel_part = lax.psum_scatter(kernel_term, "ctx", scatter_dimension=0, tiled=True)
    kernel_grad = lax.psum_scatter(kernel_part, "vid", scatter_dimension=1, tiled=True)
    return (features_grad[None], kernel_grad, mod_grads, vector_grads, latent_grad)


def solution(mesh):
    placed = (
        P("vid", "ctx", None, None, None),
        P("vid", "ctx", None, None, None),
        P("vid", None),
        P("vid", None),
        P("vid", None, None, None),
        P(),
        P(),
        P(),
        P(),
        P(),
        P(),
        P(),
    )
    return jax.shard_map(
        local,
        mesh=mesh,
        in_specs=placed,
        out_specs=(
            P("vid", "ctx", None, None, None),
            P("ctx", "vid"),
            P(),
            P(),
            P("vid", "ctx", None, None),
        ),
        check_vma=False,
    )
```

profile of v0, /device:TPU:1, one launch (start us, length us, event | category | flops | bytes accessed | tf_op | source)
XLA Modules:
  0.0 388.4 jit_solution(9092506910952850593)
XLA Ops:
  7.2 1.3 collective-permute-start
  8.8 0.9 fusion.29
  9.8 0.7 broadcast_in_dim.52
  10.6 0.7 broadcast_in_dim.54
  11.5 0.9 fusion.28
  12.6 1.2 collective-permute-done
  13.8 0.9 pad_maximum_fusion.1
  14.8 0.3 pad_slice_fusion.1
  15.0 0.9 pad_slice_fusion
  16.2 0.3 fusion.45
  16.5 0.3 fusion.44
  16.8 0.3 convolution_add_fusion.24
  17.1 0.3 convolution_add_fusion.23
  17.4 0.3 convolution_add_fusion.22
  17.7 0.3 fusion
  18.0 0.3 convolution_add_fusion.20
  18.3 0.3 convolution_add_fusion.19
  18.6 0.3 convolution_add_fusion.18
  18.9 0.3 convolution_add_fusion.17
  19.2 0.3 convolution_add_fusion.16
  19.5 0.3 convolution_add_fusion.15
  19.8 0.3 convolution_add_fusion.14
  20.1 0.3 convolution_add_fusion.13
  20.4 0.3 convolution_add_fusion.12
  20.7 0.3 convolution_add_fusion.11
  21.0 0.3 convolution_add_fusion.10
  21.3 0.3 convolution_add_fusion.9
  21.6 0.3 convolution_add_fusion.8
  21.9 0.3 convolution_add_fusion.7
  22.2 0.3 convolution_add_fusion.6
  22.5 0.3 convolution_add_fusion.5
  22.8 0.3 convolution_add_fusion.4
  23.1 0.3 convolution_add_fusion.3
  23.4 0.3 convolution_add_fusion.2
  23.7 0.3 convolution_add_fusion.1
  24.0 0.3 convolution_add_fusion
  24.6 0.5 fusion.42
  25.1 4.1 %collective-permute-start.1 = (bf16[2,8,32,256]{3,2,1,0:T(8,128)(2,1)S(1)}, bf16[2,8,32,256]{3,2,1,0:T(8,128)(2,1)S(1)}, u32[]{:S(2)}, u32[]{:S(2)}) collective-permute-start(bf16[2,8,32,256]{3,2,1,0:T(8,128)(2,1)S(1)} %get-tuple-element.26), channel_id=1, source_target_pairs={{0,8},{8,16},{16,24},{24,32},{32,40},{40,48},{48,56},{56,64},{64,7... | collective-permute-start | bytes 786440 | tf_op jit(solution)/shard_map/ppermute | solution.py:21
  29.3 3.1 collective-permute-done.1
  32.5 0.3 pad_slice_fusion.27
  32.8 0.9 pad_slice_fusion.26
  34.0 0.3 fusion.26
  34.2 0.3 fusion.25
  34.5 0.3 fusion.24
  34.8 0.3 fusion.23
  35.1 0.3 fusion.22
  35.3 0.3 fusion.21
  35.6 0.3 fusion.20
  35.9 0.3 fusion.19
  36.2 0.3 fusion.18
  36.5 0.3 fusion.17
  36.7 0.3 fusion.16
  37.0 0.3 fusion.15
  37.3 0.3 fusion.14
  41.2 1.7 copy-done.2
  42.9 5.2 %copy.25 = f32[6912,128]{0,1:T(8,128)} copy(f32[6912,128]{1,0:T(8,128)} %bitcast.425) | data formatting | bytes 7077888 | tf_op jit(solution)/shard_map/reshape | solution.py:110
  48.2 1.3 dynamic-slice.17
  50.7 3.8 collective-permute-start.2
  54.9 115.7 %all-reduce.3 = (f32[2,16,256]{2,1,0:T(8,128)}, f32[4,256]{1,0:T(4,128)}) all-reduce(f32[2,16,256]{2,1,0:T(8,128)S(1)} %pad_maximum_fusion.2, f32[4,256]{1,0:T(4,128)S(1)} %pad_maximum_fusion.3), channel_id=1, replica_groups=mesh['ctx'=64,'vid'=8] {'ctx','vid'}, use_global_device_ids=true, to_apply=%region_6.7 | all-reduce | flops 9216 | bytes 73728 | tf_op jit(solution)/shard_map/psum | solution.py:144
  170.6 0.8 fusion.38
  171.4 166.4 %all-reduce.6.cloned.1.call-done = f32[6912,128]{0,1:T(8,128)} async-done(((f32[6912,128]{0,1:T(8,128)}), f32[6912,128]{0,1:T(8,128)}) %all-reduce.6.cloned.1.call-update) | async-done | bytes 3538960
  337.8 1.6 constant_dynamic-slice_fusion.1
  339.5 0.6 fusion.55
  340.1 41.6 %reduce-scatter.3.cloned.1.call-done = f32[108,16]{0,1:T(8,128)} async-done(((f32[108,128]{0,1:T(8,128)}), f32[108,16]{0,1:T(8,128)}) %reduce-scatter.3.cloned.1.call-update) | async-done | bytes 6928 | tf_op jit(solution)/shard_map/reduce_scatter | solution.py:146
  (62 shorter events, 6.1 us)
Async XLA Ops:
  7.2 1.4 copy-start
  7.2 330.6 %all-reduce.6.cloned.1.call-start = ((), (), s32[]{:S(2)}) async-start(), calls=%async_computation.2 | async-start | bytes 7077888
  7.2 6.6 %collective-permute-start = (bf16[2,8,32,128]{3,2,1,0:T(8,128)(2,1)}, bf16[2,8,32,128]{3,2,1,0:T(8,128)(2,1)S(1)}, u32[]{:S(2)}, u32[]{:S(2)}) collective-permute-start(bf16[2,8,32,128]{3,2,1,0:T(8,128)(2,1)} %bitcast.393), channel_id=1, source_target_pairs={{8,0},{16,8},{24,16},{32,24},{40,32},{48,40},{56,48},{64,56},{72,6... | collective-permute-start | bytes 393224 | tf_op jit(solution)/shard_map/ppermute | solution.py:21
  14.7 1.5 copy-start.3
  23.7 1.0 copy-start.4
  23.7 0.9 copy-start.7
  23.7 0.9 copy-start.8
  25.1 7.2 %collective-permute-start.1 = (bf16[2,8,32,256]{3,2,1,0:T(8,128)(2,1)S(1)}, bf16[2,8,32,256]{3,2,1,0:T(8,128)(2,1)S(1)}, u32[]{:S(2)}, u32[]{:S(2)}) collective-permute-start(bf16[2,8,32,256]{3,2,1,0:T(8,128)(2,1)S(1)} %get-tuple-element.26), channel_id=1, source_target_pairs={{0,8},{8,16},{16,24},{24,32},{32,40},{40,48},{48,56},{56,64},{64,7... | collective-permute-start | bytes 786440 | tf_op jit(solution)/shard_map/ppermute | solution.py:21
  32.5 1.2 copy-start.1
  41.2 1.8 copy-start.2
  48.1 2.3 copy-start.6
  48.1 2.5 copy-start.5
  48.1 333.5 %reduce-scatter.3.cloned.1.call-start = ((), (), s32[]{:S(2)}) async-start(), calls=%async_computation.1 | async-start | bytes 73728 | tf_op jit(solution)/shard_map/reduce_scatter | solution.py:146
  50.7 288.7 %collective-permute-start.2 = (f32[16,8]{0,1:T(8,128)S(1)}, f32[16,8]{0,1:T(8,128)S(1)}, u32[]{:S(2)}, u32[]{:S(2)}) collective-permute-start(f32[16,8]{0,1:T(8,128)S(1)} %dynamic-slice_bitcast_fusion), channel_id=1, source_target_pairs={{0,8},{8,0},{16,24},{24,16},{32,40},{40,32},{48,56},{56,48},{64,72... | collective-permute-start | bytes 1544 | tf_op jit(solution)/shard_map/ppermute | solution.py:27
Sparse Core Ops, SparseCore 0:
  48.3 289.5 all-reduce.5
  341.2 40.3 reduce-scatter.2
where the time goes:
time: 390 us; the launch traced here: 388 us
  waiting for transfers between devices  212 us (54%)
  blocking collectives  116 us (30%)
  matrix products  17.6 us (5%)
  between operations  15.4 us (4%)
  local copies, waits for them, and re-layouts  15 us (4%)
  starting transfers between devices  9.3 us (2%)
    unnamed x3, waiting for transfers between devices  166 us
    psum x1, blocking collectives, local(): mod_grads, vector_grads = lax.psum((mod_part, vec_part), ('ctx', 'vid'))  116 us
    reduce_scatter x1, waiting for transfers between devices, local(): lax.psum_scatter(kernel_part, 'vid', scatter_dimension=1, tiled=True)  41.6 us
    dot_general x27, matrix products, transpose_conv(): lax.dot_general(source, tap_weights[frame_tap, row_tap, col_tap], (((1,),...  7.9 us
  transfers between devices with their start and end apart: 5, of which 4 were waited for; matrix products, arithmetic and copies ran while one was open for 2% of the time, Pallas kernels for 0%

commit v1 on v0

v1 whole, which is shorter than its diff:
```python
import jax
import jax.numpy as jnp
from jax import lax
from jax.experimental import pallas as pl
from jax.experimental.pallas import tpu as pltpu
from jax.sharding import PartitionSpec as P

MESH = pl.DeviceIdType.MESH
F32 = jnp.float32
BF16 = jnp.bfloat16
HIGHEST = lax.Precision.HIGHEST

NX, NY, NZ = 4, 4, 16
NCTX = NY * NZ
H, W, C, CO, CZ, G, LP = 8, 32, 256, 128, 16, 32, 16
PX = H * W
ROWS = 108
TILES = 10
HALF = NZ // 2
WIDE = HALF * 128


def exact(lhs, rhs, dims):
    return lax.dot_general(lhs, rhs, (dims, ((), ())), precision=HIGHEST, preferred_element_type=F32)


def wide_dot(lhs, rhs, dims):
    return lax.dot_general(lhs, rhs, (dims, ((), ())), preferred_element_type=F32)


def body(
    feat_ref, grad_ref, mean_ref, rstd_ref, lat_ref, gamma_ref, beta_ref, ws_ref, bs_ref, wh_ref, bh_ref, kern_hbm,
    fg_ref, kg_ref, mod_ref, vec_ref, lg_ref,
    kern, halo, act, dmod, norm, patch, gsum, agrad, tabs, maps, pools,
    own_a, own_b, cs_a, cs_b, cr_a, cr_b, fs_a, fs_b, fr_a, fr_b, ss_a, ss_b, sr_a, sr_b,
    zo, zs, zr, small, gathered, crossed, final, ls, lr,
    kern_sem, halo_s, halo_r, core_s, core_r, first_s, first_r, second_s, second_r, z_s, z_r,
    small_s, small_r, cross_s, cross_r, final_s, final_r, lat_s, lat_r,
):
    ctx = lax.axis_index("ctx")
    vid = lax.axis_index("vid")
    z, y = lax.div(ctx, NY), lax.rem(ctx, NY)
    x, core = lax.div(vid, 2), lax.rem(vid, 2)
    plane = y * 8 + vid

    def plane_id(p):
        return (z * NY + lax.div(p, 8), lax.rem(p, 8))

    def z_id(zz):
        return (zz * NY + y, vid)

    def x_id(xx):
        return (ctx, 2 * xx + core)

    def y_id(yy):
        return (z * NY + yy, vid)

    mate = (ctx, vid + 1 - 2 * core)
    sharer = (ctx + 1 - 2 * lax.rem(ctx, 2), vid)

    fetch = pltpu.make_async_copy(kern_hbm, kern, kern_sem)
    fetch.start()

    barrier = pltpu.get_barrier_semaphore()

    def greet(device):
        pl.semaphore_signal(barrier, inc=1, device_id=device, device_id_type=MESH)

    @pl.loop(1, 32)
    def _(k):
        greet(plane_id(lax.rem(plane + k, 32)))

    @pl.loop(1, NZ)
    def _(k):
        greet(z_id(lax.rem(z + k, NZ)))

    greet((lax.rem(ctx + 1, NCTX), vid))
    greet((lax.rem(ctx + NCTX - 1, NCTX), vid))

    def remote(src, dst, send, recv, device):
        return pltpu.make_async_remote_copy(
            src_ref=src, dst_ref=dst, send_sem=send, recv_sem=recv, device_id=device, device_id_type=MESH
        )

    pick = (lax.broadcasted_iota(jnp.int32, (G, C), 1) // (C // G) == lax.broadcasted_iota(jnp.int32, (G, C), 0)).astype(F32)
    mean_c = exact(jnp.broadcast_to(mean_ref[...], (8, G)), pick, ((1,), (0,)))[0:1]
    rstd_c = exact(jnp.broadcast_to(rstd_ref[...], (8, G)), pick, ((1,), (0,)))[0:1]
    gamma = gamma_ref[...].reshape(1, C)
    beta = beta_ref[...].reshape(1, C)
    lat = lat_ref[0, lax.div(ctx, 2)]
    scale_tab = exact(lat, ws_ref[...], ((0,), (0,))) + bs_ref[...].reshape(1, C)
    shift_tab = exact(lat, wh_ref[...], ((0,), (0,))) + bh_ref[...].reshape(1, C)
    tabs[...] = scale_tab
    pix = lax.broadcasted_iota(jnp.int32, (2 * W, LP), 0)
    latent_pixel = lax.broadcasted_iota(jnp.int32, (2 * W, LP), 1)
    spread = ((pix // W) * (W // 4) + (pix % W) // 4 == latent_pixel).astype(F32)
    scale_map = exact(spread, scale_tab, ((1,), (0,)))
    shift_map = exact(spread, shift_tab, ((1,), (0,)))
    maps[0] = scale_map.reshape(2, W, C)
    maps[1] = shift_map.reshape(2, W, C)

    @pl.loop(0, 2 * H)
    def _(i):
        f, h = lax.div(i, H), lax.rem(i, H)
        hh = lax.div(h, 4)
        normed = (feat_ref[0, f, h].astype(F32) - mean_c) * rstd_c
        modulated = (normed * gamma + beta) * maps[0, hh] + maps[1, hh]
        s = jax.nn.sigmoid(modulated)
        norm[i] = normed
        dmod[i] = s * (1.0 + modulated * (1.0 - s))
        act[pl.ds(pl.multiple_of(i * W, W), W), :] = (modulated * s).astype(BF16)

    pl.semaphore_wait(barrier, 48)
    before = (lax.rem(ctx + NCTX - 1, NCTX), vid)
    halo_copies = [
        remote(grad_ref.at[0, f], halo.at[f], halo_s.at[f], halo_r.at[f], before) for f in range(2)
    ]
    for copy in halo_copies:
        copy.start()

    col = lax.broadcasted_iota(jnp.int32, (PX, CO), 0) % W

    def lay_patches(f, g):
        for c in range(3):
            if c == 0:
                moved = jnp.where(col == W - 1, 0.0, pltpu.roll(g, PX - 1, 0))
            elif c == 1:
                moved = g
            else:
                moved = jnp.where(col == 0, 0.0, pltpu.roll(g, 1, 0))
            moved = moved.astype(BF16)
            blank = jnp.zeros((W, CO), BF16)
            for b in range(3):
                lanes = slice((b * 3 + c) * CO, (b * 3 + c + 1) * CO)
                base = f * PX
                if b == 0:
                    patch[base : base + PX - W, lanes] = moved[W:]
                    patch[base + PX - W : base + PX, lanes] = blank
                elif b == 1:
                    patch[base : base + PX, lanes] = moved
                else:
                    patch[base : base + W, lanes] = blank
                    patch[base + W : base + PX, lanes] = moved[: PX - W]

    for f in range(2):
        lay_patches(f, grad_ref[0, f].astype(F32).reshape(PX, CO))

    def filter_term(a, first, last, images):
        for bc in range(9):
            lanes = slice(bc * CO, (bc + 1) * CO)
            tap = a * 9 + bc
            yield slice(tap * C, (tap + 1) * C), wide_dot(patch[first:last, lanes], images, ((0,), (0,)))

    def taps(a):
        return jnp.concatenate([kern[(a * 9 + bc) * C : (a * 9 + bc + 1) * C, :] for bc in range(9)], axis=1)

    def input_term(a, first, last):
        return wide_dot(patch[first:last, :], taps(a), ((1,), (1,)))

    gsum[:, 27 * C :] = jnp.zeros((CO, 128), F32)
    for span, term in filter_term(2, 0, 2 * PX, act[...]):
        gsum[:, span] = term
    fetch.wait()
    agrad[...] = input_term(2, 0, 2 * PX)

    for f in range(2):
        halo_copies[f].wait_recv()
        beyond = jnp.where(ctx == NCTX - 1, 0.0, halo[f].astype(F32).reshape(PX, CO))
        lay_patches(2 + f, beyond)
    for a in (1, 0):
        for span, term in filter_term(a, (2 - a) * PX, (4 - a) * PX, act[...]):
            gsum[:, span] = term

    @pl.when(ctx == 0)
    def _():
        for span, term in filter_term(1, 0, PX, act[0:PX]):
            gsum[:, span] += term
        for f in range(2):
            for span, term in filter_term(0, f * PX, (f + 1) * PX, act[0:PX]):
                gsum[:, span] += term

    lane = lax.broadcasted_iota(jnp.int32, (CO, 128), 1)

    def deal(first_z, own, cs, x_major):
        @pl.loop(0, HALF * NY)
        def _(i):
            zl, yy = lax.div(i, NY), lax.rem(i, NY)
            start = ROWS * ((first_z + zl) * NY + yy)
            tile = lax.div(start, 128)
            off = start - tile * 128
            low = gsum[:, pl.ds(pl.multiple_of(tile * 128, 128), 128)]
            high = gsum[:, pl.ds(pl.multiple_of(tile * 128 + 128, 128), 128)]
            turn = lax.rem(128 - off, 128)
            block = jnp.where(lane < 128 - off, pltpu.roll(low, turn, 1), pltpu.roll(high, turn, 1))
            block = block.reshape(NX, 2, 16, 128)
            mine = jnp.where(core == 0, block[:, 0], block[:, 1])
            theirs = jnp.where(core == 0, block[:, 1], block[:, 0]).astype(BF16)
            lanes = pl.ds(pl.multiple_of(zl * 128, 128), 128)
            for xx in range(NX):
                if x_major:
                    own[xx, yy, :, lanes] = mine[xx]
                    cs[xx, yy, :, lanes] = theirs[xx]
                else:
                    own[yy, xx, :, lanes] = mine[xx]
                    cs[yy, xx, :, lanes] = theirs[xx]

    deal(HALF, own_a, cs_a, True)
    core_a = remote(cs_a, cr_a, core_s.at[0], core_r.at[0], mate)
    core_a.start()
    deal(0, own_b, cs_b, False)
    core_b = remote(cs_b, cr_b, core_s.at[1], core_r.at[1], mate)
    core_b.start()

    for a in (1, 0):
        agrad[...] += input_term(a, (2 - a) * PX, (4 - a) * PX)

    @pl.when(ctx == 0)
    def _():
        agrad[0:PX, :] += input_term(1, 0, PX) + input_term(0, 0, PX) + input_term(0, PX, 2 * PX)

    def pair_sum(own, cr, fs):
        @pl.loop(0, 16)
        def _(i):
            j, m = lax.div(i, 4), lax.rem(i, 4)
            total = own[j, m] + cr[j, m].astype(F32)
            own[j, m] = total
            fs[j, m] = total.astype(BF16)

    core_a.wait_recv()
    pair_sum(own_a, cr_a, fs_a)
    first_a = []
    for k in range(1, 4):
        xx = lax.rem(x + k, NX)
        first_a.append(remote(fs_a.at[xx], fr_a.at[k - 1], first_s.at[0, k - 1], first_r.at[0, k - 1], x_id(xx)))
        first_a[-1].start()
    core_b.wait_recv()
    pair_sum(own_b, cr_b, fs_b)
    first_b = []
    for k in range(1, 4):
        yy = lax.rem(y + k, NY)
        first_b.append(remote(fs_b.at[yy], fr_b.at[k - 1], first_s.at[1, k - 1], first_r.at[1, k - 1], y_id(yy)))
        first_b[-1].start()

    pools[...] = jnp.zeros_like(pools)

    @pl.loop(0, 2 * H)
    def _(i):
        f, h = lax.div(i, H), lax.rem(i, H)
        hh = lax.div(h, 4)
        pre = agrad[pl.ds(pl.multiple_of(i * W, W), W), :] * dmod[i]
        fg_ref[0, f, h] = (pre * maps[0, hh] * gamma * rstd_c).astype(BF16)
        pools[0, hh] += pre * norm[i]
        pools[1, hh] += pre

    normed_pool = exact(spread, pools[0].reshape(2 * W, C), ((0,), (0,)))
    shift_pool = exact(spread, pools[1].reshape(2 * W, C), ((0,), (0,)))
    scale_pool = normed_pool * gamma + shift_pool * beta
    tab = tabs[...]
    rows = [
        exact(lat, scale_pool, ((1,), (0,))),
        exact(lat, shift_pool, ((1,), (0,))),
        jnp.concatenate(
            [
                jnp.sum(tab * normed_pool, axis=0, keepdims=True),
                jnp.sum(tab * shift_pool, axis=0, keepdims=True),
                jnp.sum(scale_pool, axis=0, keepdims=True),
                jnp.sum(shift_pool, axis=0, keepdims=True),
                jnp.zeros((4, C), F32),
            ],
            axis=0,
        ),
    ]
    for t in range(TILES):
        block, half = t // 2, t % 2
        source = rows[block // 2][(block % 2) * 8 : (block % 2) * 8 + 8]
        small[t] = source[:, half * 128 : (half + 1) * 128]
    latent_sum = exact(ws_ref[...], scale_pool, ((1,), (1,))) + exact(wh_ref[...], shift_pool, ((1,), (1,)))
    ls[...] = jnp.zeros_like(ls)
    ls[:, 0:LP] = latent_sum
    lat_copy = remote(ls, lr, lat_s, lat_r, sharer)
    lat_copy.start()

    chip = y * NX + x
    owner = jnp.logical_and(core == 0, chip < TILES)

    def tile_plane(t):
        return lax.div(t, NX) * 8 + 2 * lax.rem(t, NX)

    @pl.loop(0, TILES)
    def _(t):
        @pl.when(tile_plane(t) != plane)
        def _():
            remote(small.at[t], gathered.at[plane], small_s.at[t], small_r.at[plane], plane_id(tile_plane(t))).start()

    def line_sum(own, place, fr, ss):
        @pl.loop(0, 4)
        def _(j):
            ss[j] = own[place, j] + fr[0, j].astype(F32) + fr[1, j].astype(F32) + fr[2, j].astype(F32)

    for copy in first_a:
        copy.wait_recv()
    line_sum(own_a, x, fr_a, ss_a)
    second_a = []
    for k in range(1, 4):
        yy = lax.rem(y + k, NY)
        second_a.append(remote(ss_a.at[yy], sr_a.at[k - 1], second_s.at[0, k - 1], second_r.at[0, k - 1], y_id(yy)))
        second_a[-1].start()
    for copy in first_b:
        copy.wait_recv()
    line_sum(own_b, y, fr_b, ss_b)
    second_b = []
    for k in range(1, 4):
        xx = lax.rem(x + k, NX)
        second_b.append(remote(ss_b.at[xx], sr_b.at[k - 1], second_s.at[1, k - 1], second_r.at[1, k - 1], x_id(xx)))
        second_b[-1].start()

    @pl.when(owner)
    def _():
        gathered[plane] = small[chip]

        @pl.loop(1, 32)
        def _(k):
            p = lax.rem(plane + k, 32)
            remote(small.at[0], gathered.at[p], small_s.at[0], small_r.at[p], plane_id(p)).wait_recv()

        crossed[z] = jnp.sum(gathered[...], axis=0)

        @pl.loop(1, NZ)
        def _(k):
            zz = lax.rem(z + k, NZ)
            remote(crossed.at[z], crossed.at[z], cross_s.at[k - 1], cross_r.at[k - 1], z_id(zz)).start()

    def settle(second, ss, place, sr, first_z):
        for copy in second:
            copy.wait_recv()
        total = ss[place] + sr[0] + sr[1] + sr[2]
        for j in range(HALF):
            piece = total[:, j * 128 : (j + 1) * 128]
            zo[first_z + j] = piece
            zs[first_z + j] = piece.astype(BF16)

    settle(second_a, ss_a, y, sr_a, HALF)
    settle(second_b, ss_b, x, sr_b, 0)

    def z_copy(k):
        zz = lax.rem(z + k, NZ)
        return remote(zs.at[zz], zr.at[k - 1], z_s.at[k - 1], z_r.at[k - 1], z_id(zz))

    @pl.loop(1, NZ)
    def _(k):
        z_copy(k).start()

    @pl.when(owner)
    def _():
        @pl.loop(1, NZ)
        def _(k):
            zz = lax.rem(z + NZ - k, NZ)
            remote(crossed.at[z], crossed.at[zz], cross_s.at[k - 1], cross_r.at[k - 1], z_id(zz)).wait_recv()

        final[chip] = jnp.sum(crossed[...], axis=0)

        @pl.loop(1, 32)
        def _(k):
            p = lax.rem(plane + k, 32)
            remote(final.at[chip], final.at[chip], final_s.at[k - 1], final_r.at[chip], plane_id(p)).start()

    @pl.loop(1, NZ)
    def _(k):
        z_copy(k).wait_recv()

    total = zo[z]
    for k in range(NZ - 1):
        total = total + zr[k].astype(F32)
    kg_ref[...] = total.T[:ROWS]

    lat_copy.wait_recv()
    both = ls[...] + lr[...]
    lg_ref[0, 0] = jnp.where(lax.rem(ctx, 2) == 0, both[:, 0 : LP // 2], both[:, LP // 2 : LP])

    @pl.loop(0, TILES)
    def _(t):
        @pl.when(tile_plane(t) != plane)
        def _():
            remote(final.at[t], final.at[t], final_s.at[0], final_r.at[t], mate).wait_recv()

    for t in range(8):
        block, half = t // 2, t % 2
        mod_ref[block // 2, (block % 2) * 8 : (block % 2) * 8 + 8, half * 128 : (half + 1) * 128] = final[t]
    for half in range(2):
        vec_ref[:, half * 128 : (half + 1) * 128] = final[8 + half, 0:4]

    for copy in halo_copies + [core_a, core_b, lat_copy] + first_a + first_b + second_a + second_b:
        copy.wait_send()

    @pl.loop(1, NZ)
    def _(k):
        z_copy(k).wait_send()

    @pl.loop(0, TILES)
    def _(t):
        @pl.when(tile_plane(t) != plane)
        def _():
            remote(small.at[t], gathered.at[plane], small_s.at[t], small_r.at[plane], plane_id(tile_plane(t))).wait_send()

    @pl.when(owner)
    def _():
        @pl.loop(1, NZ)
        def _(k):
            zz = lax.rem(z + k, NZ)
            remote(crossed.at[z], crossed.at[z], cross_s.at[k - 1], cross_r.at[k - 1], z_id(zz)).wait_send()

        @pl.loop(1, 32)
        def _(k):
            p = lax.rem(plane + k, 32)
            remote(final.at[chip], final.at[chip], final_s.at[k - 1], final_r.at[chip], plane_id(p)).wait_send()


def local(*operands):
    vmem = pl.BlockSpec(memory_space=pltpu.VMEM)
    dma = pltpu.SemaphoreType.DMA
    quad = (4, 4, 16, WIDE)
    return pl.pallas_call(
        body,
        out_shape=(
            jax.ShapeDtypeStruct((1, 2, H, W, C), BF16),
            jax.ShapeDtypeStruct((ROWS, 16), F32),
            jax.ShapeDtypeStruct((2, CZ, C), F32),
            jax.ShapeDtypeStruct((4, C), F32),
            jax.ShapeDtypeStruct((1, 1, CZ, LP // 2), F32),
        ),
        in_specs=[vmem] * 11 + [pl.BlockSpec(memory_space=pl.ANY)],
        out_specs=(vmem,) * 5,
        scratch_shapes=[
            pltpu.VMEM((27 * C, CO), BF16),
            pltpu.VMEM((2, H, W, CO), BF16),
            pltpu.VMEM((2 * PX, C), BF16),
            pltpu.VMEM((2 * H, W, C), F32),
            pltpu.VMEM((2 * H, W, C), F32),
            pltpu.VMEM((4 * PX, 9 * CO), BF16),
            pltpu.VMEM((CO, 27 * C + 128), F32),
            pltpu.VMEM((2 * PX, C), F32),
            pltpu.VMEM((LP, C), F32),
            pltpu.VMEM((2, 2, W, C), F32),
            pltpu.VMEM((2, 2, W, C), F32),
            pltpu.VMEM(quad, F32),
            pltpu.VMEM(quad, F32),
            pltpu.VMEM(quad, BF16),
            pltpu.VMEM(quad, BF16),
            pltpu.VMEM(quad, BF16),
            pltpu.VMEM(quad, BF16),
            pltpu.VMEM(quad, BF16),
            pltpu.VMEM(quad, BF16),
            pltpu.VMEM((3,) + quad[1:], BF16),
            pltpu.VMEM((3,) + quad[1:], BF16),
            pltpu.VMEM(quad[1:], F32),
            pltpu.VMEM(quad[1:], F32),
            pltpu.VMEM((3, 16, WIDE), F32),
            pltpu.VMEM((3, 16, WIDE), F32),
            pltpu.VMEM((NZ, 16, 128), F32),
            pltpu.VMEM((NZ, 16, 128), BF16),
            pltpu.VMEM((NZ - 1, 16, 128), BF16),
            pltpu.VMEM((TILES, 8, 128), F32),
            pltpu.VMEM((32, 8, 128), F32),
            pltpu.VMEM((NZ, 8, 128), F32),
            pltpu.VMEM((TILES, 8, 128), F32),
            pltpu.VMEM((16, 128), F32),
            pltpu.VMEM((16, 128), F32),
            dma,
            dma((2,)),
            dma((2,)),
            dma((2,)),
            dma((2,)),
            dma((2, 3)),
            dma((2, 3)),
            dma((2, 3)),
            dma((2, 3)),
            dma((NZ - 1,)),
            dma((NZ - 1,)),
            dma((TILES,)),
            dma((32,)),
            dma((NZ - 1,)),
            dma((NZ - 1,)),
            dma((31,)),
            dma((TILES,)),
            dma,
            dma,
        ],
        compiler_params=pltpu.CompilerParams(
            collective_id=0, has_side_effects=True, vmem_limit_bytes=60 * 1024 * 1024
        ),
    )(*operands)


def solution(mesh):
    placed = (
        P("vid", "ctx", None, None, None),
        P("vid", "ctx", None, None, None),
        P("vid", None),
        P("vid", None),
        P("vid", None, None, None),
        P(),
        P(),
        P(),
        P(),
        P(),
        P(),
        P(),
    )
    return jax.shard_map(
        local,
        mesh=mesh,
        in_specs=placed,
        out_specs=(
            P("vid", "ctx", None, None, None),
            P("ctx", "vid"),
            P(),
            P(),
            P("vid", "ctx", None, None),
        ),
        check_vma=False,
    )
```

time: 390 us -> 66.3 us (0.17)
  waiting for transfers between devices: 212 us -> 0 us
  blocking collectives: 116 us -> 0 us
  Pallas kernels: 0 us -> 56.3 us
  matrix products: 17.6 us -> 0 us
  between operations: 15.4 us -> 0.64 us
  starting transfers between devices: 9.3 us -> 0 us
  local copies, waits for them, and re-layouts: 15 us -> 8.91 us
    unnamed x3 -> x0, waiting for transfers between devices: 166 us -> none
    psum x1 -> x0, blocking collectives: 116 us -> none  [local(): mod_grads, vector_grads = lax.psum((mod_part, vec_part), ('ctx', 'vid'))]
    pallas_call x0 -> x1, Pallas kernels: none -> 56.3 us  [local(): pl.pallas_call(body, out_shape=(jax.ShapeDtypeStruct((1, 2, H, W, C), BF1...]
    reduce_scatter x1 -> x0, waiting for transfers between devices: 41.6 us -> none  [local(): lax.psum_scatter(kernel_part, 'vid', scatter_dimension=1, tiled=True)]
    dot_general x60 -> x0, matrix products: 17.6 us -> none  [the longest x27 7.9 us: transpose_conv(): lax.dot_general(source, tap_weights[frame_tap, row_tap, col_tap], (((1,),...]
    ppermute x3 -> x0, starting transfers between devices: 9.22 us -> none  [the longest x2 5.4 us: passed_along(): lax.ppermute(value, axis, [(source, source + steps) for source in range(l...]
    reshape x1 -> x0, local copies, waits for them, and re-layouts: 5.17 us -> none  [local(): kernel_term = jnp.stack(pieces).reshape(27 * C, CO)]
    ppermute x3 -> x0, waiting for transfers between devices: 4.29 us -> none  [the longest x2 4.29 us: passed_along(): lax.ppermute(value, axis, [(source, source + steps) for source in range(l...]
  transfers between devices with their start and end apart: 5 -> 0, of which waited for: 4 -> 0; matrix products, arithmetic and copies ran while one was open for 2% -> 0% of each run, Pallas kernels for 0% -> 0%
where the time goes in v1:
time: 66.3 us; the launch traced here: 65.9 us
  Pallas kernels  56.3 us (85%)
  local copies, waits for them, and re-layouts  8.91 us (13%)
    pallas_call x1, Pallas kernels, local(): pl.pallas_call(body, out_shape=(jax.ShapeDtypeStruct((1, 2, H, W, C), BF1...  56.3 us
    unnamed x4, local copies, waits for them, and re-layouts  6.06 us
    pallas_call x2, local copies, waits for them, and re-layouts, local(): pl.pallas_call(body, out_shape=(jax.ShapeDtypeStruct((1, 2, H, W, C), BF1...  2.85 us

profile of v1, /device:TPU:1, one launch (start us, length us, event | category | flops | bytes accessed | tf_op | source)
XLA Modules:
  0.0 65.9 jit_solution(17863707790583008081)
XLA Ops:
  0.6 1.8 %copy.17.lat_ref = f32[1,32,16,16]{3,2,1,0:T(8,128)} copy(f32[1,32,16,16]{1,3,2,0:T(8,128)} %param.16) | data formatting | bytes 65536 | tf_op args[4]
  2.4 56.3 %shard_map.155 = (bf16[1,2,8,32,256]{4,3,2,1,0:T(8,128)(2,1)}, f32[108,16]{1,0:T(8,128)}, f32[2,16,256]{2,1,0:T(8,128)}, f32[4,256]{1,0:T(4,128)}, f32[1,1,16,8]{3,2,1,0:T(8,128)}) custom-call(bf16[1,2,8,32,256]{4,3,2,1,0:T(8,128)(2,1)} %feat_ref.1, bf16[1,2,8,32,128]{4,3,2,1,0:T(8,128)(2,1)} %grad_ref.1, f32[1,32]{1,0:T(1,128)} %mean_ref.1, ...), custom_call_target="tpu_custom_call" | custom-call | tf_op jit(solution)/shard_map/pallas_call | solution.py:422
  58.7 1.4 %copy.19 = f32[1,1,16,8]{2,3,1,0:T(8,128)} copy(f32[1,1,16,8]{3,2,1,0:T(8,128)} %get-tuple-element.9) | data formatting | bytes 1024 | tf_op jit(solution)/shard_map/pallas_call | solution.py:422
  60.1 1.5 %copy.18 = f32[108,16]{0,1:T(8,128)} copy(f32[108,16]{1,0:T(8,128)} %get-tuple-element.6) | data formatting | bytes 13824 | tf_op jit(solution)/shard_map/pallas_call | solution.py:422
  61.6 1.7 %copy.23 = bf16[1,2,8,32,256]{4,3,2,1,0:T(8,128)(2,1)} copy(bf16[1,2,8,32,256]{4,3,2,1,0:T(8,128)(2,1)} %get-tuple-element.15) | data formatting | bytes 524288
  63.3 1.4 %copy.24 = f32[2,16,256]{2,1,0:T(8,128)} copy(f32[2,16,256]{2,1,0:T(8,128)} %get-tuple-element.17) | data formatting | bytes 65536
  64.6 1.3 %copy.25 = f32[4,256]{1,0:T(4,128)} copy(f32[4,256]{1,0:T(4,128)} %get-tuple-element.18) | data formatting | bytes 8192

commit v2 on v1

v2 whole, which is shorter than its diff:
```python
import jax
import jax.numpy as jnp
from jax import lax
from jax.experimental import pallas as pl
from jax.experimental.pallas import tpu as pltpu
from jax.sharding import PartitionSpec as P

MESH = pl.DeviceIdType.MESH
F32 = jnp.float32
BF16 = jnp.bfloat16
HIGHEST = lax.Precision.HIGHEST

NX, NY, NZ = 4, 4, 16
NCTX = NY * NZ
H, W, C, CO, CZ, G, LP = 8, 32, 256, 128, 16, 32, 16
PX = H * W
ROWS = 108
TILES = 10
PARTS = ((13, 3, "x"), (11, 2, "y"), (0, 5, "x"), (5, 6, "y"))
EARLY = 11
FAR_FIRST = (8, 7, 9, 6, 10, 5, 11, 4, 12, 3, 13, 2, 14, 1, 15)


def exact(lhs, rhs, dims):
    return lax.dot_general(lhs, rhs, (dims, ((), ())), precision=HIGHEST, preferred_element_type=F32)


def wide_dot(lhs, rhs, dims):
    return lax.dot_general(lhs, rhs, (dims, ((), ())), preferred_element_type=F32)


def body(
    feat_hbm, grad_hbm, mean_hbm, rstd_hbm, lat_hbm, gamma_hbm, beta_hbm, ws_hbm, bs_hbm, wh_hbm, bh_hbm, kern_hbm,
    fg_ref, kg_ref, final, lg_ref,
    feat_ref, grad_ref, mean_ref, rstd_ref, lat_ref, gamma_ref, beta_ref, ws_ref, bs_ref, wh_ref, bh_ref, kern,
    halo, act, dmod, norm, patch, gsum, agrad, tabs, maps, pools,
    zo, zs, zr, small, gathered, crossed, ls, lr,
    load_sems, halo_s, halo_r, core_s, core_r, first_s, first_r, second_s, second_r, z_s, z_r,
    small_s, small_r, cross_s, cross_r, final_s, final_r, lat_s, lat_r, relay,
    *part_refs,
):
    ctx = lax.axis_index("ctx")
    vid = lax.axis_index("vid")
    z, y = lax.div(ctx, NY), lax.rem(ctx, NY)
    x, core = lax.div(vid, 2), lax.rem(vid, 2)
    plane = y * 8 + vid

    def plane_id(p):
        return (z * NY + lax.div(p, 8), lax.rem(p, 8))

    def z_id(zz):
        return (zz * NY + y, vid)

    def x_id(xx):
        return (ctx, 2 * xx + core)

    def y_id(yy):
        return (z * NY + yy, vid)

    mate = (ctx, vid + 1 - 2 * core)
    sharer = (ctx + 1 - 2 * lax.rem(ctx, 2), vid)
    before = (lax.rem(ctx + NCTX - 1, NCTX), vid)
    after = (lax.rem(ctx + 1, NCTX), vid)

    loads = [
        pltpu.make_async_copy(source, target, load_sems.at[n])
        for n, (source, target) in enumerate(
            (
                (lat_hbm, lat_ref),
                (mean_hbm, mean_ref),
                (rstd_hbm, rstd_ref),
                (ws_hbm, ws_ref),
                (wh_hbm, wh_ref),
                (bs_hbm, bs_ref),
                (bh_hbm, bh_ref),
                (gamma_hbm, gamma_ref),
                (beta_hbm, beta_ref),
                (feat_hbm, feat_ref),
                (grad_hbm, grad_ref),
                (kern_hbm, kern),
            )
        )
    ]
    for load in loads:
        load.start()

    barrier = pltpu.get_barrier_semaphore()

    def signal(semaphore, device):
        pl.semaphore_signal(semaphore, inc=1, device_id=device, device_id_type=MESH)

    signal(barrier, before)
    signal(barrier, after)

    @pl.loop(1, 32)
    def _(k):
        signal(barrier, plane_id(lax.rem(plane + k, 32)))

    @pl.loop(1, 5)
    def _(k):
        signal(barrier, z_id(lax.rem(z + k, NZ)))
        signal(barrier, z_id(lax.rem(z + NZ - k, NZ)))

    def remote(src, dst, send, recv, device):
        return pltpu.make_async_remote_copy(
            src_ref=src, dst_ref=dst, send_sem=send, recv_sem=recv, device_id=device, device_id_type=MESH
        )

    for load in loads[:9]:
        load.wait()

    pick = (lax.broadcasted_iota(jnp.int32, (G, C), 1) // (C // G) == lax.broadcasted_iota(jnp.int32, (G, C), 0)).astype(F32)
    saved = jnp.concatenate([mean_ref[...], rstd_ref[...], jnp.zeros((6, G), F32)], axis=0)
    saved = exact(saved, pick, ((1,), (0,)))
    mean_c, rstd_c = saved[0:1], saved[1:2]
    gamma = gamma_ref[...].reshape(1, C)
    beta = beta_ref[...].reshape(1, C)
    here = (lax.broadcasted_iota(jnp.int32, (NCTX // 2, 128), 0) == lax.div(ctx, 2)).astype(F32)
    lat = exact(lat_ref[0].reshape(CZ * LP, NCTX // 2), here, ((1,), (0,))).reshape(CZ, LP, 128)
    corner = lax.broadcasted_iota(jnp.int32, (CZ, LP, 128), 1) == lax.broadcasted_iota(jnp.int32, (CZ, LP, 128), 2)
    lat = jnp.sum(jnp.where(corner, lat, 0.0), axis=1)[:, :LP]
    weights = jnp.concatenate([ws_ref[...], wh_ref[...]], axis=1)
    bias = jnp.concatenate([bs_ref[...].reshape(1, C), bh_ref[...].reshape(1, C)], axis=1)
    both_tabs = exact(lat, weights, ((0,), (0,))) + bias
    tabs[...] = both_tabs[:, :C]
    pix = lax.broadcasted_iota(jnp.int32, (2 * W, LP), 0)
    latent_pixel = lax.broadcasted_iota(jnp.int32, (2 * W, LP), 1)
    spread = ((pix // W) * (W // 4) + (pix % W) // 4 == latent_pixel).astype(F32)
    both_maps = exact(spread, both_tabs, ((1,), (0,)))
    maps[0] = both_maps[:, :C].reshape(2, W, C)
    maps[1] = both_maps[:, C:].reshape(2, W, C)

    loads[9].wait()

    @pl.loop(0, 2 * H, unroll=4)
    def _(i):
        f, h = lax.div(i, H), lax.rem(i, H)
        hh = lax.div(h, 4)
        normed = (feat_ref[0, f, h].astype(F32) - mean_c) * rstd_c
        modulated = (normed * gamma + beta) * maps[0, hh] + maps[1, hh]
        s = jax.nn.sigmoid(modulated)
        norm[i] = normed
        dmod[i] = s * (1.0 + modulated * (1.0 - s))
        act[pl.ds(pl.multiple_of(i * W, W), W), :] = (modulated * s).astype(BF16)

    loads[10].wait()
    pl.semaphore_wait(barrier, 41)
    halo_copies = [
        remote(grad_ref.at[0, f], halo.at[f], halo_s.at[f], halo_r.at[f], before) for f in range(2)
    ]
    for copy in halo_copies:
        copy.start()
    signal(relay, z_id(lax.rem(z + 4, NZ)))
    signal(relay, z_id(lax.rem(z + NZ - 4, NZ)))

    col = lax.broadcasted_iota(jnp.int32, (PX, CO), 0) % W

    def lay_patches(f, g):
        for c in range(3):
            if c == 0:
                moved = jnp.where(col == W - 1, 0.0, pltpu.roll(g, PX - 1, 0))
            elif c == 1:
                moved = g
            else:
                moved = jnp.where(col == 0, 0.0, pltpu.roll(g, 1, 0))
            moved = moved.astype(BF16)
            blank = jnp.zeros((W, CO), BF16)
            for b in range(3):
                lanes = slice((b * 3 + c) * CO, (b * 3 + c + 1) * CO)
                base = f * PX
                if b == 0:
                    patch[base : base + PX - W, lanes] = moved[W:]
                    patch[base + PX - W : base + PX, lanes] = blank
                elif b == 1:
                    patch[base : base + PX, lanes] = moved
                else:
                    patch[base : base + W, lanes] = blank
                    patch[base + W : base + PX, lanes] = moved[: PX - W]

    for f in range(2):
        lay_patches(f, grad_ref[0, f].astype(F32).reshape(PX, CO))

    def filter_term(a, first, last, images):
        for bc in range(9):
            lanes = slice(bc * CO, (bc + 1) * CO)
            tap = a * 9 + bc
            yield slice(tap * C, (tap + 1) * C), wide_dot(patch[first:last, lanes], images, ((0,), (0,)))

    def taps(a):
        return jnp.concatenate([kern[(a * 9 + bc) * C : (a * 9 + bc + 1) * C, :] for bc in range(9)], axis=1)

    def input_term(a, first, last):
        return wide_dot(patch[first:last, :], taps(a), ((1,), (1,)))

    lane = lax.broadcasted_iota(jnp.int32, (CO, 128), 1)
    parts = []
    for n, (first_z, count, axis) in enumerate(PARTS):
        own, cs, cr, fs, fr, ss, sr = part_refs[7 * n : 7 * n + 7]
        places = (x, y) if axis == "x" else (y, x)
        ids = (x_id, y_id) if axis == "x" else (y_id, x_id)
        parts.append(dict(n=n, first_z=first_z, count=count, axis=axis, own=own, cs=cs, cr=cr, fs=fs, fr=fr, ss=ss, sr=sr, places=places, ids=ids))

    def deal(part):
        own, cs = part["own"], part["cs"]

        @pl.loop(0, part["count"] * NY, unroll=4)
        def _(i):
            zl, yy = lax.div(i, NY), lax.rem(i, NY)
            start = ROWS * ((part["first_z"] + zl) * NY + yy)
            tile = lax.div(start, 128)
            off = start - tile * 128
            low = gsum[:, pl.ds(pl.multiple_of(tile * 128, 128), 128)]
            high = gsum[:, pl.ds(pl.multiple_of(tile * 128 + 128, 128), 128)]
            turn = lax.rem(128 - off, 128)
            block = jnp.where(lane < 128 - off, pltpu.roll(low, turn, 1), pltpu.roll(high, turn, 1))
            block = block.reshape(NX, 2, 16, 128)
            mine = jnp.where(core == 0, block[:, 0], block[:, 1])
            theirs = jnp.where(core == 0, block[:, 1], block[:, 0]).astype(BF16)
            lanes = pl.ds(pl.multiple_of(zl * 128, 128), 128)
            for xx in range(NX):
                if part["axis"] == "x":
                    own[xx, yy, :, lanes] = mine[xx]
                    cs[xx, yy, :, lanes] = theirs[xx]
                else:
                    own[yy, xx, :, lanes] = mine[xx]
                    cs[yy, xx, :, lanes] = theirs[xx]

        n = part["n"]
        part["core"] = remote(cs, part["cr"], core_s.at[n], core_r.at[n], mate)
        part["core"].start()

    def first_stage(part):
        own, cr, fs, n = part["own"], part["cr"], part["fs"], part["n"]
        part["core"].wait_recv()

        @pl.loop(0, 16, unroll=2)
        def _(i):
            j, m = lax.div(i, 4), lax.rem(i, 4)
            total = own[j, m] + cr[j, m].astype(F32)
            own[j, m] = total
            fs[j, m] = total.astype(BF16)

        part["first"] = []
        for k in (2, 1, 3):
            there = lax.rem(part["places"][0] + k, 4)
            copy = remote(fs.at[there], part["fr"].at[k - 1], first_s.at[n, k - 1], first_r.at[n, k - 1], part["ids"][0](there))
            copy.start()
            part["first"].append(copy)

    def second_stage(part):
        own, fr, ss, n = part["own"], part["fr"], part["ss"], part["n"]
        for copy in part["first"]:
            copy.wait_recv()
        place = part["places"][0]
        for j in range(4):
            ss[j] = own[place, j] + fr[0, j].astype(F32) + fr[1, j].astype(F32) + fr[2, j].astype(F32)
        part["second"] = []
        for k in (2, 1, 3):
            there = lax.rem(part["places"][1] + k, 4)
            copy = remote(ss.at[there], part["sr"].at[k - 1], second_s.at[n, k - 1], second_r.at[n, k - 1], part["ids"][1](there))
            copy.start()
            part["second"].append(copy)

    def settle(part):
        for copy in part["second"]:
            copy.wait_recv()
        sr = part["sr"]
        total = part["ss"][part["places"][1]] + sr[0] + sr[1] + sr[2]
        for j in range(part["count"]):
            piece = total[:, j * 128 : (j + 1) * 128]
            zo[part["first_z"] + j] = piece
            zs[part["first_z"] + j] = piece.astype(BF16)

    def z_copy(k):
        zz = lax.rem(z + k, NZ)
        return zz, remote(zs.at[zz], zr.at[k - 1], z_s.at[k - 1], z_r.at[k - 1], z_id(zz))

    def send_along_z(early):
        for k in FAR_FIRST:
            zz, copy = z_copy(k)

            @pl.when(zz >= EARLY if early else zz < EARLY)
            def _():
                copy.start()

    gsum[:, 27 * C :] = jnp.zeros((CO, 128), F32)
    for span, term in filter_term(2, 0, 2 * PX, act[...]):
        gsum[:, span] = term
    deal(parts[0])
    deal(parts[1])
    loads[11].wait()
    agrad[...] = input_term(2, 0, 2 * PX)
    first_stage(parts[0])
    first_stage(parts[1])

    for f in range(2):
        halo_copies[f].wait_recv()
        beyond = jnp.where(ctx == NCTX - 1, 0.0, halo[f].astype(F32).reshape(PX, CO))
        lay_patches(2 + f, beyond)
    for a in (1, 0):
        for span, term in filter_term(a, (2 - a) * PX, (4 - a) * PX, act[...]):
            gsum[:, span] = term

    @pl.when(ctx == 0)
    def _():
        for span, term in filter_term(1, 0, PX, act[0:PX]):
            gsum[:, span] += term
        for f in range(2):
            for span, term in filter_term(0, f * PX, (f + 1) * PX, act[0:PX]):
                gsum[:, span] += term

    deal(parts[2])
    deal(parts[3])
    second_stage(parts[0])
    second_stage(parts[1])
    first_stage(parts[2])
    first_stage(parts[3])

    for a in (1, 0):
        agrad[...] += input_term(a, (2 - a) * PX, (4 - a) * PX)

    @pl.when(ctx == 0)
    def _():
        agrad[0:PX, :] += input_term(1, 0, PX) + input_term(0, 0, PX) + input_term(0, PX, 2 * PX)

    pools[...] = jnp.zeros_like(pools)

    @pl.loop(0, 2 * H, unroll=4)
    def _(i):
        f, h = lax.div(i, H), lax.rem(i, H)
        hh = lax.div(h, 4)
        pre = agrad[pl.ds(pl.multiple_of(i * W, W), W), :] * dmod[i]
        fg_ref[0, f, h] = (pre * maps[0, hh] * gamma * rstd_c).astype(BF16)
        pools[0, hh] += pre * norm[i]
        pools[1, hh] += pre

    normed_pool = exact(spread, pools[0].reshape(2 * W, C), ((0,), (0,)))
    shift_pool = exact(spread, pools[1].reshape(2 * W, C), ((0,), (0,)))
    scale_pool = normed_pool * gamma + shift_pool * beta
    tab = tabs[...]
    rows = [
        exact(lat, scale_pool, ((1,), (0,))),
        exact(lat, shift_pool, ((1,), (0,))),
        jnp.concatenate(
            [
                jnp.sum(tab * normed_pool, axis=0, keepdims=True),
                jnp.sum(tab * shift_pool, axis=0, keepdims=True),
                jnp.sum(scale_pool, axis=0, keepdims=True),
                jnp.sum(shift_pool, axis=0, keepdims=True),
                jnp.zeros((4, C), F32),
            ],
            axis=0,
        ),
    ]
    for t in range(TILES):
        block, half = t // 2, t % 2
        source = rows[block // 2][(block % 2) * 8 : (block % 2) * 8 + 8]
        small[t] = source[:, half * 128 : (half + 1) * 128]

    chip = y * NX + x
    owner = jnp.logical_and(core == 0, chip < TILES)

    def tile_plane(t):
        return lax.div(t, NX) * 8 + 2 * lax.rem(t, NX)

    @pl.loop(0, TILES)
    def _(t):
        @pl.when(tile_plane(t) != plane)
        def _():
            remote(small.at[t], gathered.at[plane], small_s.at[t], small_r.at[plane], plane_id(tile_plane(t))).start()

    latent_sum = exact(scale_pool, ws_ref[...], ((1,), (1,))) + exact(shift_pool, wh_ref[...], ((1,), (1,)))
    ls[...] = jnp.zeros_like(ls)
    ls[:, 0:CZ] = latent_sum
    lat_copy = remote(ls, lr, lat_s, lat_r, sharer)
    lat_copy.start()

    settle(parts[0])
    settle(parts[1])
    pl.semaphore_wait(relay, 2)
    send_along_z(True)
    second_stage(parts[2])
    second_stage(parts[3])

    @pl.when(owner)
    def _():
        gathered[plane] = small[chip]

        @pl.loop(1, 32)
        def _(k):
            p = lax.rem(plane + k, 32)
            remote(small.at[0], gathered.at[p], small_s.at[0], small_r.at[p], plane_id(p)).wait_recv()

        crossed[z] = jnp.sum(gathered[...], axis=0)

        @pl.loop(1, NZ)
        def _(k):
            zz = lax.rem(z + k, NZ)
            remote(crossed.at[z], crossed.at[z], cross_s.at[k - 1], cross_r.at[k - 1], z_id(zz)).start()

    settle(parts[2])
    settle(parts[3])
    send_along_z(False)

    @pl.when(owner)
    def _():
        @pl.loop(1, NZ)
        def _(k):
            zz = lax.rem(z + NZ - k, NZ)
            remote(crossed.at[z], crossed.at[zz], cross_s.at[k - 1], cross_r.at[k - 1], z_id(zz)).wait_recv()

        final[chip] = jnp.sum(crossed[...], axis=0)

        @pl.loop(1, 32)
        def _(k):
            p = lax.rem(plane + k, 32)
            remote(final.at[chip], final.at[chip], final_s.at[k - 1], final_r.at[chip], plane_id(p)).start()

    lat_copy.wait_recv()
    half = pl.ds(pl.multiple_of(lax.rem(ctx, 2) * 8, 8), 8)
    lg_ref[...] = ls[half, :] + lr[half, :]

    for k in range(1, NZ):
        z_copy(k)[1].wait_recv()
    total = zo[z]
    for k in range(NZ - 1):
        total = total + zr[k].astype(F32)
    kg_ref[...] = total

    @pl.loop(0, TILES)
    def _(t):
        @pl.when(tile_plane(t) != plane)
        def _():
            remote(final.at[t], final.at[t], final_s.at[0], final_r.at[t], mate).wait_recv()

    for copy in halo_copies + [lat_copy]:
        copy.wait_send()
    for part in parts:
        for copy in [part["core"]] + part["first"] + part["second"]:
            copy.wait_send()
    for k in range(1, NZ):
        z_copy(k)[1].wait_send()

    @pl.loop(0, TILES)
    def _(t):
        @pl.when(tile_plane(t) != plane)
        def _():
            remote(small.at[t], gathered.at[plane], small_s.at[t], small_r.at[plane], plane_id(tile_plane(t))).wait_send()

    @pl.when(owner)
    def _():
        @pl.loop(1, NZ)
        def _(k):
            zz = lax.rem(z + k, NZ)
            remote(crossed.at[z], crossed.at[z], cross_s.at[k - 1], cross_r.at[k - 1], z_id(zz)).wait_send()

        @pl.loop(1, 32)
        def _(k):
            p = lax.rem(plane + k, 32)
            remote(final.at[chip], final.at[chip], final_s.at[k - 1], final_r.at[chip], plane_id(p)).wait_send()


def finish(fg_in, kg_in, sums, lg_in, fg_ref, kg_ref, mod_ref, vec_ref, lg_ref):
    fg_ref[...] = fg_in[...]
    kg_ref[...] = kg_in[:, 0:ROWS]
    for t in range(8):
        block, half = t // 2, t % 2
        mod_ref[block // 2, (block % 2) * 8 : (block % 2) * 8 + 8, half * 128 : (half + 1) * 128] = sums[t]
    for half in range(2):
        vec_ref[:, half * 128 : (half + 1) * 128] = sums[8 + half, 0:4]
    lg_ref[0, 0] = lg_in[:, 0:CZ]


def local(features, grad_out, mean_saved, rstd_saved, latent, *others):
    operands = (features, grad_out, mean_saved, rstd_saved, jnp.transpose(latent, (0, 2, 3, 1))) + others
    vmem = pl.BlockSpec(memory_space=pltpu.VMEM)
    dma = pltpu.SemaphoreType.DMA
    buffers = []
    for _, count, _ in PARTS:
        wide = (16, count * 128)
        buffers += [
            pltpu.VMEM((4, 4) + wide, F32),
            pltpu.VMEM((4, 4) + wide, BF16),
            pltpu.VMEM((4, 4) + wide, BF16),
            pltpu.VMEM((4, 4) + wide, BF16),
            pltpu.VMEM((3, 4) + wide, BF16),
            pltpu.VMEM((4,) + wide, F32),
            pltpu.VMEM((3,) + wide, F32),
        ]
    parts = len(PARTS)
    partial = pl.pallas_call(
        body,
        out_shape=(
            jax.ShapeDtypeStruct((1, 2, H, W, C), BF16),
            jax.ShapeDtypeStruct((16, 128), F32),
            jax.ShapeDtypeStruct((TILES, 8, 128), F32),
            jax.ShapeDtypeStruct((8, 128), F32),
        ),
        in_specs=[pl.BlockSpec(memory_space=pltpu.HBM)] * 12,
        out_specs=(vmem,) * 4,
        scratch_shapes=[
            pltpu.VMEM((1, 2, H, W, C), BF16),
            pltpu.VMEM((1, 2, H, W, CO), BF16),
            pltpu.VMEM((1, G), F32),
            pltpu.VMEM((1, G), F32),
            pltpu.VMEM((1, CZ, LP, NCTX // 2), F32),
            pltpu.VMEM((C,), F32),
            pltpu.VMEM((C,), F32),
            pltpu.VMEM((CZ, C), F32),
            pltpu.VMEM((C,), F32),
            pltpu.VMEM((CZ, C), F32),
            pltpu.VMEM((C,), F32),
            pltpu.VMEM((27 * C, CO), BF16),
            pltpu.VMEM((2, H, W, CO), BF16),
            pltpu.VMEM((2 * PX, C), BF16),
            pltpu.VMEM((2 * H, W, C), F32),
            pltpu.VMEM((2 * H, W, C), F32),
            pltpu.VMEM((4 * PX, 9 * CO), BF16),
            pltpu.VMEM((CO, 27 * C + 128), F32),
            pltpu.VMEM((2 * PX, C), F32),
            pltpu.VMEM((LP, C), F32),
            pltpu.VMEM((2, 2, W, C), F32),
            pltpu.VMEM((2, 2, W, C), F32),
            pltpu.VMEM((NZ, 16, 128), F32),
            pltpu.VMEM((NZ, 16, 128), BF16),
            pltpu.VMEM((NZ - 1, 16, 128), BF16),
            pltpu.VMEM((TILES, 8, 128), F32),
            pltpu.VMEM((32, 8, 128), F32),
            pltpu.VMEM((NZ, 8, 128), F32),
            pltpu.VMEM((16, 128), F32),
            pltpu.VMEM((16, 128), F32),
            dma((12,)),
            dma((2,)),
            dma((2,)),
            dma((parts,)),
            dma((parts,)),
            dma((parts, 3)),
            dma((parts, 3)),
            dma((parts, 3)),
            dma((parts, 3)),
            dma((NZ - 1,)),
            dma((NZ - 1,)),
            dma((TILES,)),
            dma((32,)),
            dma((NZ - 1,)),
            dma((NZ - 1,)),
            dma((31,)),
            dma((TILES,)),
            dma,
            dma,
            pltpu.SemaphoreType.REGULAR,
        ]
        + buffers,
        compiler_params=pltpu.CompilerParams(
            collective_id=0, has_side_effects=True, vmem_limit_bytes=36 * 1024 * 1024
        ),
    )(*(pltpu.with_memory_space_constraint(value, pltpu.HBM) for value in operands))
    fg, kg, mod, vec, lg = pl.pallas_call(
        finish,
        out_shape=(
            jax.ShapeDtypeStruct((1, 2, H, W, C), BF16),
            jax.ShapeDtypeStruct((16, ROWS), F32),
            jax.ShapeDtypeStruct((2, CZ, C), F32),
            jax.ShapeDtypeStruct((4, C), F32),
            jax.ShapeDtypeStruct((1, 1, LP // 2, CZ), F32),
        ),
        in_specs=[vmem] * 4,
        out_specs=(vmem,) * 5,
        compiler_params=pltpu.CompilerParams(vmem_limit_bytes=8 * 1024 * 1024),
    )(*partial)
    return fg, kg.T, mod, vec, jnp.swapaxes(lg, 2, 3)


def solution(mesh):
    placed = (
        P("vid", "ctx", None, None, None),
        P("vid", "ctx", None, None, None),
        P("vid", None),
        P("vid", None),
        P("vid", None, None, None),
        P(),
        P(),
        P(),
        P(),
        P(),
        P(),
        P(),
    )
    return jax.shard_map(
        local,
        mesh=mesh,
        in_specs=placed,
        out_specs=(
            P("vid", "ctx", None, None, None),
            P("ctx", "vid"),
            P(),
            P(),
            P("vid", "ctx", None, None),
        ),
        check_vma=False,
    )
```

time: 66.3 us -> 49.7 us (0.75)
  local copies, waits for them, and re-layouts: 8.91 us -> 0 us
  Pallas kernels: 56.3 us -> 48.9 us
    pallas_call x1, Pallas kernels: 56.3 us -> 48.2 us  [local(): pl.pallas_call(body, out_shape=(jax.ShapeDtypeStruct((1, 2, H, W, C), BF1...]
    unnamed x4 -> x0, local copies, waits for them, and re-layouts: 6.06 us -> none
    pallas_call x2 -> x0, local copies, waits for them, and re-layouts: 2.85 us -> none  [local(): pl.pallas_call(body, out_shape=(jax.ShapeDtypeStruct((1, 2, H, W, C), BF1...]
    pallas_call x0 -> x1, Pallas kernels: none -> 0.74 us  [local(): pl.pallas_call(finish, out_shape=(jax.ShapeDtypeStruct((1, 2, H, W, C), B...]
where the time goes in v2:
time: 49.7 us; the launch traced here: 49.6 us
  Pallas kernels  48.9 us (98%)
  between operations  0.64 us (1%)
    pallas_call x1, Pallas kernels, local(): pl.pallas_call(body, out_shape=(jax.ShapeDtypeStruct((1, 2, H, W, C), BF1...  48.2 us

profile of v2, /device:TPU:1, one launch (start us, length us, event | category | flops | bytes accessed | tf_op | source)
XLA Modules:
  0.0 49.6 jit_solution(14451184203229940003)
XLA Ops:
  0.6 48.2 %shard_map.155 = (bf16[1,2,8,32,256]{4,3,2,1,0:T(8,128)(2,1)S(1)}, f32[16,128]{1,0:T(8,128)S(1)}, f32[10,8,128]{2,1,0:T(8,128)S(1)}, f32[8,128]{1,0:T(8,128)S(1)}) custom-call(bf16[1,2,8,32,256]{4,3,2,1,0:T(8,128)(2,1)} %feat_hbm.1, bf16[1,2,8,32,128]{4,3,2,1,0:T(8,128)(2,1)} %grad_hbm.1, f32[1,32]{1,0:T(1,128)} %mean_hbm.1, f32[1,32]{1,0:T(1,128)} %rstd_hbm.1, ...), custom_call_target="tpu_custom_call" | custom-call | tf_op jit(solution)/shard_map/pallas_call | solution.py:491
  48.8 0.7 %shard_map.156 = (bf16[1,2,8,32,256]{4,3,2,1,0:T(8,128)(2,1)}, f32[16,108]{1,0:T(8,128)}, f32[2,16,256]{2,1,0:T(8,128)}, f32[4,256]{1,0:T(4,128)}, f32[1,1,8,16]{3,2,1,0:T(8,128)}) custom-call(bf16[1,2,8,32,256]{4,3,2,1,0:T(8,128)(2,1)S(1)} %get-tuple-element.14.fg_in, f32[16,128]{1,0:T(8,128)S(1)} %get-tuple-element.15.kg_in, ...), custom_call_target="tpu_custom_call" | custom-call | tf_op jit(solution)/shard_map/pallas_call | solution.py:558

commit v3 on v2

--- a/solution.py
+++ b/solution.py
@@ -16,9 +16,15 @@
 PX = H * W
 ROWS = 108
 TILES = 10
-PARTS = ((13, 3, "x"), (11, 2, "y"), (0, 5, "x"), (5, 6, "y"))
-EARLY = 11
+PARTS = ((11, 5, "x"), (9, 2, "x"), (6, 3, "y"), (0, 3, "x"), (3, 3, "y"))
+GROUPS = ((11, 16), (6, 11), (0, 6))
 FAR_FIRST = (8, 7, 9, 6, 10, 5, 11, 4, 12, 3, 13, 2, 14, 1, 15)
+
+
+def span_of(first_z, count):
+    low = ROWS * NY * first_z // 128
+    high = -(-ROWS * NY * (first_z + count) // 128)
+    return low * 128, high * 128
 
 
 def exact(lhs, rhs, dims):
@@ -36,7 +42,7 @@
     halo, act, dmod, norm, patch, gsum, agrad, tabs, maps, pools,
     zo, zs, zr, small, gathered, crossed, ls, lr,
     load_sems, halo_s, halo_r, core_s, core_r, first_s, first_r, second_s, second_r, z_s, z_r,
-    small_s, small_r, cross_s, cross_r, final_s, final_r, lat_s, lat_r, relay,
+    small_s, small_r, cross_s, cross_r, final_s, final_r, lat_s, lat_r, relay, relay_far,
     *part_refs,
 ):
     ctx = lax.axis_index("ctx")
@@ -91,20 +97,26 @@
 
     signal(barrier, before)
     signal(barrier, after)
-
-    @pl.loop(1, 32)
-    def _(k):
-        signal(barrier, plane_id(lax.rem(plane + k, 32)))
-
-    @pl.loop(1, 5)
-    def _(k):
+    signal(barrier, mate)
+    for k in range(1, 4):
+        signal(barrier, x_id(lax.rem(x + k, NX)))
+        signal(barrier, y_id(lax.rem(y + k, NY)))
+    for k in (2, NZ - 2, 1, NZ - 1):
         signal(barrier, z_id(lax.rem(z + k, NZ)))
-        signal(barrier, z_id(lax.rem(z + NZ - k, NZ)))
 
     def remote(src, dst, send, recv, device):
         return pltpu.make_async_remote_copy(
             src_ref=src, dst_ref=dst, send_sem=send, recv_sem=recv, device_id=device, device_id_type=MESH
         )
+
+    pl.semaphore_wait(barrier, 13)
+    halo_copies = [
+        remote(grad_hbm.at[0, f], halo.at[f], halo_s.at[f], halo_r.at[f], before) for f in range(2)
+    ]
+    for copy in halo_copies:
+        copy.start()
+    signal(relay, z_id(lax.rem(z + 2, NZ)))
+    signal(relay, z_id(lax.rem(z + NZ - 2, NZ)))
 
     for load in loads[:9]:
         load.wait()
@@ -144,15 +156,6 @@
         act[pl.ds(pl.multiple_of(i * W, W), W), :] = (modulated * s).astype(BF16)
 
     loads[10].wait()
-    pl.semaphore_wait(barrier, 41)
-    halo_copies = [
-        remote(grad_ref.at[0, f], halo.at[f], halo_s.at[f], halo_r.at[f], before) for f in range(2)
-    ]
-    for copy in halo_copies:
-        copy.start()
-    signal(relay, z_id(lax.rem(z + 4, NZ)))
-    signal(relay, z_id(lax.rem(z + NZ - 4, NZ)))
-
     col = lax.broadcasted_iota(jnp.int32, (PX, CO), 0) % W
 
     def lay_patches(f, g):
@@ -192,53 +195,65 @@
     def input_term(a, first, last):
         return wide_dot(patch[first:last, :], taps(a), ((1,), (1,)))
 
-    lane = lax.broadcasted_iota(jnp.int32, (CO, 128), 1)
+    lane = lax.broadcasted_iota(jnp.int32, (16, 128), 1)
     parts = []
+    refs = list(part_refs)
     for n, (first_z, count, axis) in enumerate(PARTS):
-        own, cs, cr, fs, fr, ss, sr = part_refs[7 * n : 7 * n + 7]
         places = (x, y) if axis == "x" else (y, x)
         ids = (x_id, y_id) if axis == "x" else (y_id, x_id)
-        parts.append(dict(n=n, first_z=first_z, count=count, axis=axis, own=own, cs=cs, cr=cr, fs=fs, fr=fr, ss=ss, sr=sr, places=places, ids=ids))
+        names = ("own", "cs", "cr", "fs", "fr", "ss", "sr")
+        part = dict(zip(names, refs[:7]))
+        del refs[:7]
+        part.update(n=n, first_z=first_z, count=count, axis=axis, places=places, ids=ids)
+        parts.append(part)
+
+    def owned(place, parity):
+        return pl.ds(pl.multiple_of((2 * place + parity) * 16, 16), 16)
+
+    def shifted(low, high, off, turn):
+        return jnp.where(lane < 128 - off, pltpu.roll(low, turn, 1), pltpu.roll(high, turn, 1))
 
     def deal(part):
-        own, cs = part["own"], part["cs"]
-
-        @pl.loop(0, part["count"] * NY, unroll=4)
-        def _(i):
-            zl, yy = lax.div(i, NY), lax.rem(i, NY)
-            start = ROWS * ((part["first_z"] + zl) * NY + yy)
-            tile = lax.div(start, 128)
-            off = start - tile * 128
-            low = gsum[:, pl.ds(pl.multiple_of(tile * 128, 128), 128)]
-            high = gsum[:, pl.ds(pl.multiple_of(tile * 128 + 128, 128), 128)]
-            turn = lax.rem(128 - off, 128)
-            block = jnp.where(lane < 128 - off, pltpu.roll(low, turn, 1), pltpu.roll(high, turn, 1))
-            block = block.reshape(NX, 2, 16, 128)
-            mine = jnp.where(core == 0, block[:, 0], block[:, 1])
-            theirs = jnp.where(core == 0, block[:, 1], block[:, 0]).astype(BF16)
-            lanes = pl.ds(pl.multiple_of(zl * 128, 128), 128)
+        own, cs, n = part["own"], part["cs"], part["n"]
+        if part["axis"] == "x":
+            low, high = span_of(part["first_z"], part["count"])
             for xx in range(NX):
-                if part["axis"] == "x":
-                    own[xx, yy, :, lanes] = mine[xx]
-                    cs[xx, yy, :, lanes] = theirs[xx]
-                else:
-                    own[yy, xx, :, lanes] = mine[xx]
-                    cs[yy, xx, :, lanes] = theirs[xx]
-
-        n = part["n"]
+                cs[xx] = gsum[owned(xx, 1 - core), low:high].astype(BF16)
+        else:
+
+            @pl.loop(0, part["count"] * NY, unroll=4)
+            def _(i):
+                zl, yy = lax.div(i, NY), lax.rem(i, NY)
+                start = ROWS * ((part["first_z"] + zl) * NY + yy)
+                tile = lax.div(start, 128)
+                off = start - tile * 128
+                turn = lax.rem(128 - off, 128)
+                first = pl.ds(pl.multiple_of(tile * 128, 128), 128)
+                second = pl.ds(pl.multiple_of(tile * 128 + 128, 128), 128)
+                lanes = pl.ds(pl.multiple_of(zl * 128, 128), 128)
+                for xx in range(NX):
+                    mine, theirs = owned(xx, core), owned(xx, 1 - core)
+                    cs[yy, xx, :, lanes] = shifted(gsum[theirs, first], gsum[theirs, second], off, turn).astype(BF16)
+                    own[yy, xx, :, lanes] = shifted(gsum[mine, first], gsum[mine, second], off, turn)
+
         part["core"] = remote(cs, part["cr"], core_s.at[n], core_r.at[n], mate)
         part["core"].start()
 
     def first_stage(part):
         own, cr, fs, n = part["own"], part["cr"], part["fs"], part["n"]
         part["core"].wait_recv()
-
-        @pl.loop(0, 16, unroll=2)
-        def _(i):
-            j, m = lax.div(i, 4), lax.rem(i, 4)
-            total = own[j, m] + cr[j, m].astype(F32)
-            own[j, m] = total
-            fs[j, m] = total.astype(BF16)
+        if part["axis"] == "x":
+            low, high = span_of(part["first_z"], part["count"])
+            for xx in range(NX):
+                fs[xx] = (gsum[owned(xx, core), low:high] + cr[xx].astype(F32)).astype(BF16)
+        else:
+
+            @pl.loop(0, 16, unroll=2)
+            def _(i):
+                j, m = lax.div(i, 4), lax.rem(i, 4)
+                total = own[j, m] + cr[j, m].astype(F32)
+                own[j, m] = total
+                fs[j, m] = total.astype(BF16)
 
         part["first"] = []
         for k in (2, 1, 3):
@@ -248,12 +263,31 @@
             part["first"].append(copy)
 
     def second_stage(part):
-        own, fr, ss, n = part["own"], part["fr"], part["ss"], part["n"]
+        own, cr, fr, ss, n = part["own"], part["cr"], part["fr"], part["ss"], part["n"]
         for copy in part["first"]:
             copy.wait_recv()
-        place = part["places"][0]
-        for j in range(4):
-            ss[j] = own[place, j] + fr[0, j].astype(F32) + fr[1, j].astype(F32) + fr[2, j].astype(F32)
+        if part["axis"] == "x":
+            low, high = span_of(part["first_z"], part["count"])
+            width = high - low
+            own[:, 0:width] = (
+                gsum[owned(x, core), low:high]
+                + cr[x].astype(F32)
+                + fr[0].astype(F32)
+                + fr[1].astype(F32)
+                + fr[2].astype(F32)
+            )
+            own[:, width:] = jnp.zeros((16, 128), F32)
+            for i in range(part["count"] * NY):
+                zl, yy = i // NY, i % NY
+                start = ROWS * (part["first_z"] * NY + i) - low
+                tile, off = start // 128, start % 128
+                block = own[:, tile * 128 : tile * 128 + 128]
+                if off:
+                    block = shifted(block, own[:, tile * 128 + 128 : tile * 128 + 256], off, 128 - off)
+                ss[yy, :, zl * 128 : zl * 128 + 128] = block
+        else:
+            for j in range(4):
+                ss[j] = own[y, j] + fr[0, j].astype(F32) + fr[1, j].astype(F32) + fr[2, j].astype(F32)
         part["second"] = []
         for k in (2, 1, 3):
             there = lax.rem(part["places"][1] + k, 4)
@@ -275,11 +309,11 @@
         zz = lax.rem(z + k, NZ)
         return zz, remote(zs.at[zz], zr.at[k - 1], z_s.at[k - 1], z_r.at[k - 1], z_id(zz))
 
-    def send_along_z(early):
+    def send_along_z(first, last):
         for k in FAR_FIRST:
             zz, copy = z_copy(k)
 
-            @pl.when(zz >= EARLY if early else zz < EARLY)
+            @pl.when(jnp.logical_and(zz >= first, zz < last))
             def _():
                 copy.start()
 
@@ -287,41 +321,49 @@
     for span, term in filter_term(2, 0, 2 * PX, act[...]):
         gsum[:, span] = term
     deal(parts[0])
-    deal(parts[1])
+    for span, term in filter_term(1, PX, 2 * PX, act[0:PX]):
+        gsum[:, span] = term
     loads[11].wait()
     agrad[...] = input_term(2, 0, 2 * PX)
+    agrad[0:PX, :] += input_term(1, PX, 2 * PX)
+    pl.semaphore_wait(relay, 2)
+    signal(relay_far, z_id(lax.rem(z + 4, NZ)))
+    signal(relay_far, z_id(lax.rem(z + NZ - 4, NZ)))
     first_stage(parts[0])
-    first_stage(parts[1])
-
-    for f in range(2):
-        halo_copies[f].wait_recv()
-        beyond = jnp.where(ctx == NCTX - 1, 0.0, halo[f].astype(F32).reshape(PX, CO))
-        lay_patches(2 + f, beyond)
-    for a in (1, 0):
-        for span, term in filter_term(a, (2 - a) * PX, (4 - a) * PX, act[...]):
-            gsum[:, span] = term
 
     @pl.when(ctx == 0)
     def _():
         for span, term in filter_term(1, 0, PX, act[0:PX]):
             gsum[:, span] += term
-        for f in range(2):
-            for span, term in filter_term(0, f * PX, (f + 1) * PX, act[0:PX]):
-                gsum[:, span] += term
-
+        for span, term in filter_term(0, 0, PX, act[0:PX]):
+            gsum[:, span] = term
+        for span, term in filter_term(0, PX, 2 * PX, act[0:PX]):
+            gsum[:, span] += term
+        agrad[0:PX, :] += input_term(1, 0, PX) + input_term(0, 0, PX) + input_term(0, PX, 2 * PX)
+
+    @pl.when(ctx != 0)
+    def _():
+        gsum[:, 0 : 9 * C] = jnp.zeros((CO, 9 * C), F32)
+
+    def take_halo(f):
+        halo_copies[f].wait_recv()
+        lay_patches(2 + f, jnp.where(ctx == NCTX - 1, 0.0, halo[f].astype(F32).reshape(PX, CO)))
+
+    take_halo(0)
+    for span, term in filter_term(1, 2 * PX, 3 * PX, act[PX : 2 * PX]):
+        gsum[:, span] += term
+    deal(parts[1])
     deal(parts[2])
+    take_halo(1)
+    for span, term in filter_term(0, 2 * PX, 4 * PX, act[...]):
+        gsum[:, span] += term
     deal(parts[3])
-    second_stage(parts[0])
-    second_stage(parts[1])
-    first_stage(parts[2])
-    first_stage(parts[3])
-
-    for a in (1, 0):
-        agrad[...] += input_term(a, (2 - a) * PX, (4 - a) * PX)
-
-    @pl.when(ctx == 0)
-    def _():
-        agrad[0:PX, :] += input_term(1, 0, PX) + input_term(0, 0, PX) + input_term(0, PX, 2 * PX)
+    deal(parts[4])
+    for part in parts[1:]:
+        first_stage(part)
+
+    agrad[...] += input_term(0, 2 * PX, 4 * PX)
+    agrad[PX : 2 * PX, :] += input_term(1, 2 * PX, 3 * PX)
 
     pools[...] = jnp.zeros_like(pools)
 
@@ -363,6 +405,8 @@
     def tile_plane(t):
         return lax.div(t, NX) * 8 + 2 * lax.rem(t, NX)
 
+    second_stage(parts[0])
+
     @pl.loop(0, TILES)
     def _(t):
         @pl.when(tile_plane(t) != plane)
@@ -375,12 +419,13 @@
     lat_copy = remote(ls, lr, lat_s, lat_r, sharer)
     lat_copy.start()
 
-    settle(parts[0])
-    settle(parts[1])
-    pl.semaphore_wait(relay, 2)
-    send_along_z(True)
+    second_stage(parts[1])
     second_stage(parts[2])
     second_stage(parts[3])
+    second_stage(parts[4])
+    settle(parts[0])
+    pl.semaphore_wait(relay_far, 2)
+    send_along_z(*GROUPS[0])
 
     @pl.when(owner)
     def _():
@@ -398,9 +443,12 @@
             zz = lax.rem(z + k, NZ)
             remote(crossed.at[z], crossed.at[z], cross_s.at[k - 1], cross_r.at[k - 1], z_id(zz)).start()
 
+    settle(parts[1])
     settle(parts[2])
+    send_along_z(*GROUPS[1])
     settle(parts[3])
-    send_along_z(False)
+    settle(parts[4])
+    send_along_z(*GROUPS[2])
 
     @pl.when(owner)
     def _():
@@ -476,14 +524,16 @@
     vmem = pl.BlockSpec(memory_space=pltpu.VMEM)
     dma = pltpu.SemaphoreType.DMA
     buffers = []
-    for _, count, _ in PARTS:
+    for first_z, count, axis in PARTS:
         wide = (16, count * 128)
+        low, high = span_of(first_z, count)
+        first = (16, high - low) if axis == "x" else (4,) + wide
         buffers += [
-            pltpu.VMEM((4, 4) + wide, F32),
-            pltpu.VMEM((4, 4) + wide, BF16),
-            pltpu.VMEM((4, 4) + wide, BF16),
-            pltpu.VMEM((4, 4) + wide, BF16),
-            pltpu.VMEM((3, 4) + wide, BF16),
+            pltpu.VMEM((16, high - low + 128) if axis == "x" else (4,) + first, F32),
+            pltpu.VMEM((4,) + first, BF16),
+            pltpu.VMEM((4,) + first, BF16),
+            pltpu.VMEM((4,) + first, BF16),
+            pltpu.VMEM((3,) + first, BF16),
             pltpu.VMEM((4,) + wide, F32),
             pltpu.VMEM((3,) + wide, F32),
         ]
@@ -549,6 +599,7 @@
             dma,
             dma,
             pltpu.SemaphoreType.REGULAR,
+            pltpu.SemaphoreType.REGULAR,
         ]
         + buffers,
         compiler_params=pltpu.CompilerParams(

time: 49.7 us -> 48.5 us (0.976)
  Pallas kernels: 48.9 us -> 47.7 us
    pallas_call x1, Pallas kernels: 48.2 us -> 47 us  [local(): pl.pallas_call(body, out_shape=(jax.ShapeDtypeStruct((1, 2, H, W, C), BF1...]
where the time goes in v3:
time: 48.5 us; the launch traced here: 48.4 us
  Pallas kernels  47.7 us (98%)
  between operations  0.64 us (1%)
    pallas_call x1, Pallas kernels, local(): pl.pallas_call(body, out_shape=(jax.ShapeDtypeStruct((1, 2, H, W, C), BF1...  47 us

profile of v3, /device:TPU:1, one launch (start us, length us, event | category | flops | bytes accessed | tf_op | source)
XLA Modules:
  0.0 48.4 jit_solution(12946204026647857106)
XLA Ops:
  0.6 47.0 %shard_map.155 = (bf16[1,2,8,32,256]{4,3,2,1,0:T(8,128)(2,1)S(1)}, f32[16,128]{1,0:T(8,128)S(1)}, f32[10,8,128]{2,1,0:T(8,128)S(1)}, f32[8,128]{1,0:T(8,128)S(1)}) custom-call(bf16[1,2,8,32,256]{4,3,2,1,0:T(8,128)(2,1)} %feat_hbm.1, bf16[1,2,8,32,128]{4,3,2,1,0:T(8,128)(2,1)} %grad_hbm.1, f32[1,32]{1,0:T(1,128)} %mean_hbm.1, f32[1,32]{1,0:T(1,128)} %rstd_hbm.1, ...), custom_call_target="tpu_custom_call" | custom-call | tf_op jit(solution)/shard_map/pallas_call | solution.py:541
  47.6 0.7 %shard_map.156 = (bf16[1,2,8,32,256]{4,3,2,1,0:T(8,128)(2,1)}, f32[16,108]{1,0:T(8,128)}, f32[2,16,256]{2,1,0:T(8,128)}, f32[4,256]{1,0:T(4,128)}, f32[1,1,8,16]{3,2,1,0:T(8,128)}) custom-call(bf16[1,2,8,32,256]{4,3,2,1,0:T(8,128)(2,1)S(1)} %get-tuple-element.14.fg_in, f32[16,128]{1,0:T(8,128)S(1)} %get-tuple-element.15.kg_in, ...), custom_call_target="tpu_custom_call" | custom-call | tf_op jit(solution)/shard_map/pallas_call | solution.py:609

commit v4 on v3

--- a/solution.py
+++ b/solution.py
@@ -42,7 +42,7 @@
     halo, act, dmod, norm, patch, gsum, agrad, tabs, maps, pools,
     zo, zs, zr, small, gathered, crossed, ls, lr,
     load_sems, halo_s, halo_r, core_s, core_r, first_s, first_r, second_s, second_r, z_s, z_r,
-    small_s, small_r, cross_s, cross_r, final_s, final_r, lat_s, lat_r, relay, relay_far,
+    small_s, small_r, cross_s, cross_r, final_s, final_r, lat_s, lat_r, relay, relay_far, relay_plane, relay_mate, image, image_s,
     *part_refs,
 ):
     ctx = lax.axis_index("ctx")
@@ -117,6 +117,8 @@
         copy.start()
     signal(relay, z_id(lax.rem(z + 2, NZ)))
     signal(relay, z_id(lax.rem(z + NZ - 2, NZ)))
+    for k in range(1, 4):
+        signal(relay_plane, y_id(lax.rem(y + k, NY)))
 
     for load in loads[:9]:
         load.wait()
@@ -329,6 +331,8 @@
     pl.semaphore_wait(relay, 2)
     signal(relay_far, z_id(lax.rem(z + 4, NZ)))
     signal(relay_far, z_id(lax.rem(z + NZ - 4, NZ)))
+    pl.semaphore_wait(relay_plane, 3)
+    signal(relay_mate, mate)
     first_stage(parts[0])
 
     @pl.when(ctx == 0)
@@ -355,13 +359,6 @@
     deal(parts[1])
     deal(parts[2])
     take_halo(1)
-    for span, term in filter_term(0, 2 * PX, 4 * PX, act[...]):
-        gsum[:, span] += term
-    deal(parts[3])
-    deal(parts[4])
-    for part in parts[1:]:
-        first_stage(part)
-
     agrad[...] += input_term(0, 2 * PX, 4 * PX)
     agrad[PX : 2 * PX, :] += input_term(1, 2 * PX, 3 * PX)
 
@@ -372,10 +369,12 @@
         f, h = lax.div(i, H), lax.rem(i, H)
         hh = lax.div(h, 4)
         pre = agrad[pl.ds(pl.multiple_of(i * W, W), W), :] * dmod[i]
-        fg_ref[0, f, h] = (pre * maps[0, hh] * gamma * rstd_c).astype(BF16)
+        image[0, f, h] = (pre * maps[0, hh] * gamma * rstd_c).astype(BF16)
         pools[0, hh] += pre * norm[i]
         pools[1, hh] += pre
 
+    write_image = pltpu.make_async_copy(image, fg_ref, image_s)
+    write_image.start()
     normed_pool = exact(spread, pools[0].reshape(2 * W, C), ((0,), (0,)))
     shift_pool = exact(spread, pools[1].reshape(2 * W, C), ((0,), (0,)))
     scale_pool = normed_pool * gamma + shift_pool * beta
@@ -405,7 +404,7 @@
     def tile_plane(t):
         return lax.div(t, NX) * 8 + 2 * lax.rem(t, NX)
 
-    second_stage(parts[0])
+    pl.semaphore_wait(relay_mate, 1)
 
     @pl.loop(0, TILES)
     def _(t):
@@ -413,35 +412,43 @@
         def _():
             remote(small.at[t], gathered.at[plane], small_s.at[t], small_r.at[plane], plane_id(tile_plane(t))).start()
 
+    for span, term in filter_term(0, 2 * PX, 4 * PX, act[...]):
+        gsum[:, span] += term
+    deal(parts[3])
+    deal(parts[4])
+    for part in parts[1:]:
+        first_stage(part)
+
+    second_stage(parts[0])
     latent_sum = exact(scale_pool, ws_ref[...], ((1,), (1,))) + exact(shift_pool, wh_ref[...], ((1,), (1,)))
     ls[...] = jnp.zeros_like(ls)
     ls[:, 0:CZ] = latent_sum
     lat_copy = remote(ls, lr, lat_s, lat_r, sharer)
     lat_copy.start()
 
+    pl.semaphore_wait(relay_far, 2)
+    @pl.when(owner)
+    def _():
+        gathered[plane] = small[chip]
+
+        @pl.loop(1, 32)
+        def _(k):
+            p = lax.rem(plane + k, 32)
+            remote(small.at[0], gathered.at[p], small_s.at[0], small_r.at[p], plane_id(p)).wait_recv()
+
+        crossed[z] = jnp.sum(gathered[...], axis=0)
+
+        @pl.loop(1, NZ)
+        def _(k):
+            zz = lax.rem(z + k, NZ)
+            remote(crossed.at[z], crossed.at[z], cross_s.at[k - 1], cross_r.at[k - 1], z_id(zz)).start()
+
     second_stage(parts[1])
     second_stage(parts[2])
     second_stage(parts[3])
     second_stage(parts[4])
     settle(parts[0])
-    pl.semaphore_wait(relay_far, 2)
     send_along_z(*GROUPS[0])
-
-    @pl.when(owner)
-    def _():
-        gathered[plane] = small[chip]
-
-        @pl.loop(1, 32)
-        def _(k):
-            p = lax.rem(plane + k, 32)
-            remote(small.at[0], gathered.at[p], small_s.at[0], small_r.at[p], plane_id(p)).wait_recv()
-
-        crossed[z] = jnp.sum(gathered[...], axis=0)
-
-        @pl.loop(1, NZ)
-        def _(k):
-            zz = lax.rem(z + k, NZ)
-            remote(crossed.at[z], crossed.at[z], cross_s.at[k - 1], cross_r.at[k - 1], z_id(zz)).start()
 
     settle(parts[1])
     settle(parts[2])
@@ -481,6 +488,7 @@
         def _():
             remote(final.at[t], final.at[t], final_s.at[0], final_r.at[t], mate).wait_recv()
 
+    write_image.wait()
     for copy in halo_copies + [lat_copy]:
         copy.wait_send()
     for part in parts:
@@ -547,7 +555,7 @@
             jax.ShapeDtypeStruct((8, 128), F32),
         ),
         in_specs=[pl.BlockSpec(memory_space=pltpu.HBM)] * 12,
-        out_specs=(vmem,) * 4,
+        out_specs=(pl.BlockSpec(memory_space=pl.ANY),) + (vmem,) * 3,
         scratch_shapes=[
             pltpu.VMEM((1, 2, H, W, C), BF16),
             pltpu.VMEM((1, 2, H, W, CO), BF16),
@@ -600,6 +608,10 @@
             dma,
             pltpu.SemaphoreType.REGULAR,
             pltpu.SemaphoreType.REGULAR,
+            pltpu.SemaphoreType.REGULAR,
+            pltpu.SemaphoreType.REGULAR,
+            pltpu.VMEM((1, 2, H, W, C), BF16),
+            dma,
         ]
         + buffers,
         compiler_params=pltpu.CompilerParams(

time: 48.5 us -> 43.7 us (0.901)
  Pallas kernels: 47.7 us -> 42.7 us
    pallas_call x1, Pallas kernels: 47 us -> 42 us  [local(): pl.pallas_call(body, out_shape=(jax.ShapeDtypeStruct((1, 2, H, W, C), BF1...]
where the time goes in v4:
time: 43.7 us; the launch traced here: 43.4 us
  Pallas kernels  42.7 us (98%)
  between operations  0.64 us (1%)
    pallas_call x1, Pallas kernels, local(): pl.pallas_call(body, out_shape=(jax.ShapeDtypeStruct((1, 2, H, W, C), BF1...  42 us

profile of v4, /device:TPU:1, one launch (start us, length us, event | category | flops | bytes accessed | tf_op | source)
XLA Modules:
  0.0 43.4 jit_solution(2608888381732609915)
XLA Ops:
  0.6 42.0 %shard_map.155 = (bf16[1,2,8,32,256]{4,3,2,1,0:T(8,128)(2,1)S(1)}, f32[16,128]{1,0:T(8,128)S(1)}, f32[10,8,128]{2,1,0:T(8,128)S(1)}, f32[8,128]{1,0:T(8,128)S(1)}) custom-call(bf16[1,2,8,32,256]{4,3,2,1,0:T(8,128)(2,1)} %feat_hbm.1, bf16[1,2,8,32,128]{4,3,2,1,0:T(8,128)(2,1)} %grad_hbm.1, f32[1,32]{1,0:T(1,128)} %mean_hbm.1, f32[1,32]{1,0:T(1,128)} %rstd_hbm.1, ...), custom_call_target="tpu_custom_call" | custom-call | tf_op jit(solution)/shard_map/pallas_call | solution.py:549
  42.6 0.7 %shard_map.156 = (bf16[1,2,8,32,256]{4,3,2,1,0:T(8,128)(2,1)}, f32[16,108]{1,0:T(8,128)}, f32[2,16,256]{2,1,0:T(8,128)}, f32[4,256]{1,0:T(4,128)}, f32[1,1,8,16]{3,2,1,0:T(8,128)}) custom-call(bf16[1,2,8,32,256]{4,3,2,1,0:T(8,128)(2,1)S(1)} %get-tuple-element.14.fg_in, f32[16,128]{1,0:T(8,128)S(1)} %get-tuple-element.15.kg_in, ...), custom_call_target="tpu_custom_call" | custom-call | tf_op jit(solution)/shard_map/pallas_call | solution.py:621

commit v5 on v4

--- a/solution.py
+++ b/solution.py
@@ -16,7 +16,7 @@
 PX = H * W
 ROWS = 108
 TILES = 10
-PARTS = ((11, 5, "x"), (9, 2, "x"), (6, 3, "y"), (0, 3, "x"), (3, 3, "y"))
+PARTS = ((11, 5, "x"), (6, 3, "x"), (9, 2, "y"), (0, 3, "x"), (3, 3, "y"))
 GROUPS = ((11, 16), (6, 11), (0, 6))
 FAR_FIRST = (8, 7, 9, 6, 10, 5, 11, 4, 12, 3, 13, 2, 14, 1, 15)
 
@@ -111,7 +111,7 @@
 
     pl.semaphore_wait(barrier, 13)
     halo_copies = [
-        remote(grad_hbm.at[0, f], halo.at[f], halo_s.at[f], halo_r.at[f], before) for f in range(2)
+        remote(grad_hbm.at[0, f], halo.at[f], halo_s, halo_r.at[f], before) for f in range(2)
     ]
     for copy in halo_copies:
         copy.start()
@@ -203,9 +203,9 @@
     for n, (first_z, count, axis) in enumerate(PARTS):
         places = (x, y) if axis == "x" else (y, x)
         ids = (x_id, y_id) if axis == "x" else (y_id, x_id)
-        names = ("own", "cs", "cr", "fs", "fr", "ss", "sr")
-        part = dict(zip(names, refs[:7]))
-        del refs[:7]
+        names = ("own", "cs", "cr", "fs", "fr", "line", "ss", "sr")
+        part = dict(zip(names, refs[: len(names)]))
+        del refs[: len(names)]
         part.update(n=n, first_z=first_z, count=count, axis=axis, places=places, ids=ids)
         parts.append(part)
 
@@ -219,8 +219,10 @@
         own, cs, n = part["own"], part["cs"], part["n"]
         if part["axis"] == "x":
             low, high = span_of(part["first_z"], part["count"])
-            for xx in range(NX):
-                cs[xx] = gsum[owned(xx, 1 - core), low:high].astype(BF16)
+            part["core"] = [
+                remote(gsum.at[owned(xx, 1 - core), low:high], part["cr"].at[xx], core_s.at[n], core_r.at[n], mate)
+                for xx in range(NX)
+            ]
         else:
 
             @pl.loop(0, part["count"] * NY, unroll=4)
@@ -235,45 +237,45 @@
                 lanes = pl.ds(pl.multiple_of(zl * 128, 128), 128)
                 for xx in range(NX):
                     mine, theirs = owned(xx, core), owned(xx, 1 - core)
-                    cs[yy, xx, :, lanes] = shifted(gsum[theirs, first], gsum[theirs, second], off, turn).astype(BF16)
+                    cs[yy, xx, :, lanes] = shifted(gsum[theirs, first], gsum[theirs, second], off, turn)
                     own[yy, xx, :, lanes] = shifted(gsum[mine, first], gsum[mine, second], off, turn)
 
-        part["core"] = remote(cs, part["cr"], core_s.at[n], core_r.at[n], mate)
-        part["core"].start()
+            part["core"] = [remote(cs, part["cr"], core_s.at[n], core_r.at[n], mate)]
+        for copy in part["core"]:
+            copy.start()
 
     def first_stage(part):
         own, cr, fs, n = part["own"], part["cr"], part["fs"], part["n"]
-        part["core"].wait_recv()
+        remote(cr, cr, core_s.at[n], core_r.at[n], mate).wait_recv()
         if part["axis"] == "x":
             low, high = span_of(part["first_z"], part["count"])
             for xx in range(NX):
-                fs[xx] = (gsum[owned(xx, core), low:high] + cr[xx].astype(F32)).astype(BF16)
+                fs[xx] = (gsum[owned(xx, core), low:high] + cr[xx]).astype(BF16)
         else:
 
             @pl.loop(0, 16, unroll=2)
             def _(i):
                 j, m = lax.div(i, 4), lax.rem(i, 4)
-                total = own[j, m] + cr[j, m].astype(F32)
+                total = own[j, m] + cr[j, m]
                 own[j, m] = total
                 fs[j, m] = total.astype(BF16)
 
         part["first"] = []
         for k in (2, 1, 3):
             there = lax.rem(part["places"][0] + k, 4)
-            copy = remote(fs.at[there], part["fr"].at[k - 1], first_s.at[n, k - 1], first_r.at[n, k - 1], part["ids"][0](there))
+            copy = remote(fs.at[there], part["fr"].at[k - 1], first_s.at[n], first_r.at[n], part["ids"][0](there))
             copy.start()
             part["first"].append(copy)
 
     def second_stage(part):
-        own, cr, fr, ss, n = part["own"], part["cr"], part["fr"], part["ss"], part["n"]
-        for copy in part["first"]:
-            copy.wait_recv()
+        own, cr, fr, line, ss, n = part["own"], part["cr"], part["fr"], part["line"], part["ss"], part["n"]
+        remote(fr, fr, first_s.at[n], first_r.at[n], mate).wait_recv()
         if part["axis"] == "x":
             low, high = span_of(part["first_z"], part["count"])
             width = high - low
             own[:, 0:width] = (
                 gsum[owned(x, core), low:high]
-                + cr[x].astype(F32)
+                + cr[x]
                 + fr[0].astype(F32)
                 + fr[1].astype(F32)
                 + fr[2].astype(F32)
@@ -286,22 +288,23 @@
                 block = own[:, tile * 128 : tile * 128 + 128]
                 if off:
                     block = shifted(block, own[:, tile * 128 + 128 : tile * 128 + 256], off, 128 - off)
-                ss[yy, :, zl * 128 : zl * 128 + 128] = block
+                line[yy, :, zl * 128 : zl * 128 + 128] = block
         else:
             for j in range(4):
-                ss[j] = own[y, j] + fr[0, j].astype(F32) + fr[1, j].astype(F32) + fr[2, j].astype(F32)
+                line[j] = own[y, j] + fr[0, j].astype(F32) + fr[1, j].astype(F32) + fr[2, j].astype(F32)
+        for j in range(4):
+            ss[j] = line[j].astype(BF16)
         part["second"] = []
         for k in (2, 1, 3):
             there = lax.rem(part["places"][1] + k, 4)
-            copy = remote(ss.at[there], part["sr"].at[k - 1], second_s.at[n, k - 1], second_r.at[n, k - 1], part["ids"][1](there))
+            copy = remote(ss.at[there], part["sr"].at[k - 1], second_s.at[n], second_r.at[n], part["ids"][1](there))
             copy.start()
             part["second"].append(copy)
 
     def settle(part):
-        for copy in part["second"]:
-            copy.wait_recv()
-        sr = part["sr"]
-        total = part["ss"][part["places"][1]] + sr[0] + sr[1] + sr[2]
+        sr, n = part["sr"], part["n"]
+        remote(sr, sr, second_s.at[n], second_r.at[n], mate).wait_recv()
+        total = part["line"][part["places"][1]] + sr[0].astype(F32) + sr[1].astype(F32) + sr[2].astype(F32)
         for j in range(part["count"]):
             piece = total[:, j * 128 : (j + 1) * 128]
             zo[part["first_z"] + j] = piece
@@ -309,7 +312,7 @@
 
     def z_copy(k):
         zz = lax.rem(z + k, NZ)
-        return zz, remote(zs.at[zz], zr.at[k - 1], z_s.at[k - 1], z_r.at[k - 1], z_id(zz))
+        return zz, remote(zs.at[zz], zr.at[k - 1], z_s, z_r, z_id(zz))
 
     def send_along_z(first, last):
         for k in FAR_FIRST:
@@ -410,13 +413,15 @@
     def _(t):
         @pl.when(tile_plane(t) != plane)
         def _():
-            remote(small.at[t], gathered.at[plane], small_s.at[t], small_r.at[plane], plane_id(tile_plane(t))).start()
-
+            remote(small.at[t], gathered.at[plane], small_s, small_r, plane_id(tile_plane(t))).start()
+
+    first_stage(parts[1])
+    first_stage(parts[2])
     for span, term in filter_term(0, 2 * PX, 4 * PX, act[...]):
         gsum[:, span] += term
     deal(parts[3])
     deal(parts[4])
-    for part in parts[1:]:
+    for part in parts[3:]:
         first_stage(part)
 
     second_stage(parts[0])
@@ -429,19 +434,16 @@
     pl.semaphore_wait(relay_far, 2)
     @pl.when(owner)
     def _():
+        others = gathered.at[0:31]
+        remote(others, others, small_s, small_r, mate).wait_recv()
+
         gathered[plane] = small[chip]
-
-        @pl.loop(1, 32)
-        def _(k):
-            p = lax.rem(plane + k, 32)
-            remote(small.at[0], gathered.at[p], small_s.at[0], small_r.at[p], plane_id(p)).wait_recv()
-
         crossed[z] = jnp.sum(gathered[...], axis=0)
 
         @pl.loop(1, NZ)
         def _(k):
             zz = lax.rem(z + k, NZ)
-            remote(crossed.at[z], crossed.at[z], cross_s.at[k - 1], cross_r.at[k - 1], z_id(zz)).start()
+            remote(crossed.at[z], crossed.at[z], cross_s, cross_r, z_id(zz)).start()
 
     second_stage(parts[1])
     second_stage(parts[2])
@@ -459,61 +461,56 @@
 
     @pl.when(owner)
     def _():
-        @pl.loop(1, NZ)
-        def _(k):
-            zz = lax.rem(z + NZ - k, NZ)
-            remote(crossed.at[z], crossed.at[zz], cross_s.at[k - 1], cross_r.at[k - 1], z_id(zz)).wait_recv()
-
+        others = crossed.at[0 : NZ - 1]
+        remote(others, others, cross_s, cross_r, mate).wait_recv()
         final[chip] = jnp.sum(crossed[...], axis=0)
 
         @pl.loop(1, 32)
         def _(k):
             p = lax.rem(plane + k, 32)
-            remote(final.at[chip], final.at[chip], final_s.at[k - 1], final_r.at[chip], plane_id(p)).start()
+            remote(final.at[chip], final.at[chip], final_s, final_r, plane_id(p)).start()
 
     lat_copy.wait_recv()
     half = pl.ds(pl.multiple_of(lax.rem(ctx, 2) * 8, 8), 8)
     lg_ref[...] = ls[half, :] + lr[half, :]
 
-    for k in range(1, NZ):
-        z_copy(k)[1].wait_recv()
+    remote(zr, zr, z_s, z_r, mate).wait_recv()
     total = zo[z]
     for k in range(NZ - 1):
         total = total + zr[k].astype(F32)
     kg_ref[...] = total
 
-    @pl.loop(0, TILES)
-    def _(t):
-        @pl.when(tile_plane(t) != plane)
-        def _():
-            remote(final.at[t], final.at[t], final_s.at[0], final_r.at[t], mate).wait_recv()
+    @pl.when(owner)
+    def _():
+        others = final.at[0 : TILES - 1]
+        remote(others, others, final_s, final_r, mate).wait_recv()
+
+    @pl.when(jnp.logical_not(owner))
+    def _():
+        remote(final, final, final_s, final_r, mate).wait_recv()
 
     write_image.wait()
-    for copy in halo_copies + [lat_copy]:
-        copy.wait_send()
+    remote(halo, halo, halo_s, halo_r.at[0], mate).wait_send()
+    lat_copy.wait_send()
     for part in parts:
-        for copy in [part["core"]] + part["first"] + part["second"]:
-            copy.wait_send()
-    for k in range(1, NZ):
-        z_copy(k)[1].wait_send()
-
-    @pl.loop(0, TILES)
-    def _(t):
-        @pl.when(tile_plane(t) != plane)
-        def _():
-            remote(small.at[t], gathered.at[plane], small_s.at[t], small_r.at[plane], plane_id(tile_plane(t))).wait_send()
+        n = part["n"]
+        remote(part["cr"], part["cr"], core_s.at[n], core_r.at[n], mate).wait_send()
+        remote(part["fr"], part["fr"], first_s.at[n], first_r.at[n], mate).wait_send()
+        remote(part["sr"], part["sr"], second_s.at[n], second_r.at[n], mate).wait_send()
+    remote(zr, zr, z_s, z_r, mate).wait_send()
 
     @pl.when(owner)
     def _():
-        @pl.loop(1, NZ)
-        def _(k):
-            zz = lax.rem(z + k, NZ)
-            remote(crossed.at[z], crossed.at[z], cross_s.at[k - 1], cross_r.at[k - 1], z_id(zz)).wait_send()
-
-        @pl.loop(1, 32)
-        def _(k):
-            p = lax.rem(plane + k, 32)
-            remote(final.at[chip], final.at[chip], final_s.at[k - 1], final_r.at[chip], plane_id(p)).wait_send()
+        tiles = small.at[0 : TILES - 1]
+        remote(tiles, tiles, small_s, small_r, mate).wait_send()
+        places = crossed.at[0 : NZ - 1]
+        remote(places, places, cross_s, cross_r, mate).wait_send()
+        copies = gathered.at[0:31]
+        remote(copies, copies, final_s, final_r, mate).wait_send()
+
+    @pl.when(jnp.logical_not(owner))
+    def _():
+        remote(small, small, small_s, small_r, mate).wait_send()
 
 
 def finish(fg_in, kg_in, sums, lg_in, fg_ref, kg_ref, mod_ref, vec_ref, lg_ref):
@@ -538,12 +535,13 @@
         first = (16, high - low) if axis == "x" else (4,) + wide
         buffers += [
             pltpu.VMEM((16, high - low + 128) if axis == "x" else (4,) + first, F32),
-            pltpu.VMEM((4,) + first, BF16),
-            pltpu.VMEM((4,) + first, BF16),
+            pltpu.VMEM((8, 128) if axis == "x" else (4,) + first, F32),
+            pltpu.VMEM((4,) + first, F32),
             pltpu.VMEM((4,) + first, BF16),
             pltpu.VMEM((3,) + first, BF16),
             pltpu.VMEM((4,) + wide, F32),
-            pltpu.VMEM((3,) + wide, F32),
+            pltpu.VMEM((4,) + wide, BF16),
+            pltpu.VMEM((3,) + wide, BF16),
         ]
     parts = len(PARTS)
     partial = pl.pallas_call(
@@ -588,22 +586,22 @@
             pltpu.VMEM((16, 128), F32),
             pltpu.VMEM((16, 128), F32),
             dma((12,)),
-            dma((2,)),
+            dma,
             dma((2,)),
             dma((parts,)),
             dma((parts,)),
-            dma((parts, 3)),
-            dma((parts, 3)),
-            dma((parts, 3)),
-            dma((parts, 3)),
-            dma((NZ - 1,)),
-            dma((NZ - 1,)),
-            dma((TILES,)),
-            dma((32,)),
-            dma((NZ - 1,)),
-            dma((NZ - 1,)),
-            dma((31,)),
-            dma((TILES,)),
+            dma((parts,)),
+            dma((parts,)),
+            dma((parts,)),
+            dma((parts,)),
+            dma,
+            dma,
+            dma,
+            dma,
+            dma,
+            dma,
+            dma,
+            dma,
             dma,
             dma,
             pltpu.SemaphoreType.REGULAR,

time: 43.7 us -> 41.5 us (0.950)
  Pallas kernels: 42.7 us -> 40.7 us
    pallas_call x1, Pallas kernels: 42 us -> 40 us  [local(): pl.pallas_call(body, out_shape=(jax.ShapeDtypeStruct((1, 2, H, W, C), BF1...]
where the time goes in v5:
time: 41.5 us; the launch traced here: 41.4 us
  Pallas kernels  40.7 us (98%)
  between operations  0.64 us (2%)
    pallas_call x1, Pallas kernels, local(): pl.pallas_call(body, out_shape=(jax.ShapeDtypeStruct((1, 2, H, W, C), BF1...  40 us

profile of v5, /device:TPU:1, one launch (start us, length us, event | category | flops | bytes accessed | tf_op | source)
XLA Modules:
  0.0 41.4 jit_solution(15844688304832645892)
XLA Ops:
  0.6 40.0 %shard_map.155 = (bf16[1,2,8,32,256]{4,3,2,1,0:T(8,128)(2,1)S(1)}, f32[16,128]{1,0:T(8,128)S(1)}, f32[10,8,128]{2,1,0:T(8,128)S(1)}, f32[8,128]{1,0:T(8,128)S(1)}) custom-call(bf16[1,2,8,32,256]{4,3,2,1,0:T(8,128)(2,1)} %feat_hbm.1, bf16[1,2,8,32,128]{4,3,2,1,0:T(8,128)(2,1)} %grad_hbm.1, f32[1,32]{1,0:T(1,128)} %mean_hbm.1, f32[1,32]{1,0:T(1,128)} %rstd_hbm.1, ...), custom_call_target="tpu_custom_call" | custom-call | tf_op jit(solution)/shard_map/pallas_call | solution.py:547
  40.6 0.7 %shard_map.156 = (bf16[1,2,8,32,256]{4,3,2,1,0:T(8,128)(2,1)}, f32[16,108]{1,0:T(8,128)}, f32[2,16,256]{2,1,0:T(8,128)}, f32[4,256]{1,0:T(4,128)}, f32[1,1,8,16]{3,2,1,0:T(8,128)}) custom-call(bf16[1,2,8,32,256]{4,3,2,1,0:T(8,128)(2,1)S(1)} %get-tuple-element.14.fg_in, f32[16,128]{1,0:T(8,128)S(1)} %get-tuple-element.15.kg_in, ...), custom_call_target="tpu_custom_call" | custom-call | tf_op jit(solution)/shard_map/pallas_call | solution.py:619

commit v6 on v5

--- a/solution.py
+++ b/solution.py
@@ -42,7 +42,7 @@
     halo, act, dmod, norm, patch, gsum, agrad, tabs, maps, pools,
     zo, zs, zr, small, gathered, crossed, ls, lr,
     load_sems, halo_s, halo_r, core_s, core_r, first_s, first_r, second_s, second_r, z_s, z_r,
-    small_s, small_r, cross_s, cross_r, final_s, final_r, lat_s, lat_r, relay, relay_far, relay_plane, relay_mate, image, image_s,
+    small_s, small_r, cross_s, cross_r, final_s, final_r, lat_s, lat_r, relay, relay_far, relay_plane, relay_mate, image, image_s, turned,
     *part_refs,
 ):
     ctx = lax.axis_index("ctx")
@@ -191,11 +191,13 @@
             tap = a * 9 + bc
             yield slice(tap * C, (tap + 1) * C), wide_dot(patch[first:last, lanes], images, ((0,), (0,)))
 
-    def taps(a):
-        return jnp.concatenate([kern[(a * 9 + bc) * C : (a * 9 + bc + 1) * C, :] for bc in range(9)], axis=1)
+    def turn_taps(a):
+        for bc in range(9):
+            tap = a * 9 + bc
+            turned[a, bc * CO : (bc + 1) * CO, :] = kern[tap * C : (tap + 1) * C, :].T
 
     def input_term(a, first, last):
-        return wide_dot(patch[first:last, :], taps(a), ((1,), (1,)))
+        return wide_dot(patch[first:last, :], turned[a], ((1,), (0,)))
 
     lane = lax.broadcasted_iota(jnp.int32, (16, 128), 1)
     parts = []
@@ -329,6 +331,8 @@
     for span, term in filter_term(1, PX, 2 * PX, act[0:PX]):
         gsum[:, span] = term
     loads[11].wait()
+    for a in (2, 1, 0):
+        turn_taps(a)
     agrad[...] = input_term(2, 0, 2 * PX)
     agrad[0:PX, :] += input_term(1, PX, 2 * PX)
     pl.semaphore_wait(relay, 2)
@@ -378,13 +382,15 @@
 
     write_image = pltpu.make_async_copy(image, fg_ref, image_s)
     write_image.start()
-    normed_pool = exact(spread, pools[0].reshape(2 * W, C), ((0,), (0,)))
-    shift_pool = exact(spread, pools[1].reshape(2 * W, C), ((0,), (0,)))
+    fields = jnp.concatenate([pools[0].reshape(2 * W, C), pools[1].reshape(2 * W, C)], axis=1)
+    pooled = exact(spread, fields, ((0,), (0,)))
+    normed_pool, shift_pool = pooled[:, :C], pooled[:, C:]
     scale_pool = normed_pool * gamma + shift_pool * beta
+    projected = exact(lat, jnp.concatenate([scale_pool, shift_pool], axis=1), ((1,), (0,)))
     tab = tabs[...]
     rows = [
-        exact(lat, scale_pool, ((1,), (0,))),
-        exact(lat, shift_pool, ((1,), (0,))),
+        projected[:, :C],
+        projected[:, C:],
         jnp.concatenate(
             [
                 jnp.sum(tab * normed_pool, axis=0, keepdims=True),
@@ -431,6 +437,8 @@
     lat_copy = remote(ls, lr, lat_s, lat_r, sharer)
     lat_copy.start()
 
+    second_stage(parts[1])
+    second_stage(parts[2])
     pl.semaphore_wait(relay_far, 2)
     @pl.when(owner)
     def _():
@@ -445,8 +453,6 @@
             zz = lax.rem(z + k, NZ)
             remote(crossed.at[z], crossed.at[z], cross_s, cross_r, z_id(zz)).start()
 
-    second_stage(parts[1])
-    second_stage(parts[2])
     second_stage(parts[3])
     second_stage(parts[4])
     settle(parts[0])
@@ -610,6 +616,7 @@
             pltpu.SemaphoreType.REGULAR,
             pltpu.VMEM((1, 2, H, W, C), BF16),
             dma,
+            pltpu.VMEM((3, 9 * CO, C), BF16),
         ]
         + buffers,
         compiler_params=pltpu.CompilerParams(

time: 41.5 us -> 41.5 us (level)
  no operation moved by 1% of the time
where the time goes in v6:
time: 41.5 us; the launch traced here: 41.3 us
  Pallas kernels  40.7 us (98%)
  between operations  0.64 us (2%)
    pallas_call x1, Pallas kernels, local(): pl.pallas_call(body, out_shape=(jax.ShapeDtypeStruct((1, 2, H, W, C), BF1...  40 us

profile of v6, /device:TPU:1, one launch (start us, length us, event | category | flops | bytes accessed | tf_op | source)
XLA Modules:
  0.0 41.3 jit_solution(9688056937199255755)
XLA Ops:
  0.6 40.0 %shard_map.155 = (bf16[1,2,8,32,256]{4,3,2,1,0:T(8,128)(2,1)S(1)}, f32[16,128]{1,0:T(8,128)S(1)}, f32[10,8,128]{2,1,0:T(8,128)S(1)}, f32[8,128]{1,0:T(8,128)S(1)}) custom-call(bf16[1,2,8,32,256]{4,3,2,1,0:T(8,128)(2,1)} %feat_hbm.1, bf16[1,2,8,32,128]{4,3,2,1,0:T(8,128)(2,1)} %grad_hbm.1, f32[1,32]{1,0:T(1,128)} %mean_hbm.1, f32[1,32]{1,0:T(1,128)} %rstd_hbm.1, ...), custom_call_target="tpu_custom_call" | custom-call | tf_op jit(solution)/shard_map/pallas_call | solution.py:553
  40.6 0.7 %shard_map.156 = (bf16[1,2,8,32,256]{4,3,2,1,0:T(8,128)(2,1)}, f32[16,108]{1,0:T(8,128)}, f32[2,16,256]{2,1,0:T(8,128)}, f32[4,256]{1,0:T(4,128)}, f32[1,1,8,16]{3,2,1,0:T(8,128)}) custom-call(bf16[1,2,8,32,256]{4,3,2,1,0:T(8,128)(2,1)S(1)} %get-tuple-element.14.fg_in, f32[16,128]{1,0:T(8,128)S(1)} %get-tuple-element.15.kg_in, ...), custom_call_target="tpu_custom_call" | custom-call | tf_op jit(solution)/shard_map/pallas_call | solution.py:626

commit v7 on v6

--- a/solution.py
+++ b/solution.py
@@ -421,10 +421,10 @@
         def _():
             remote(small.at[t], gathered.at[plane], small_s, small_r, plane_id(tile_plane(t))).start()
 
+    for span, term in filter_term(0, 2 * PX, 4 * PX, act[...]):
+        gsum[:, span] += term
     first_stage(parts[1])
     first_stage(parts[2])
-    for span, term in filter_term(0, 2 * PX, 4 * PX, act[...]):
-        gsum[:, span] += term
     deal(parts[3])
     deal(parts[4])
     for part in parts[3:]:
@@ -461,10 +461,6 @@
     settle(parts[1])
     settle(parts[2])
     send_along_z(*GROUPS[1])
-    settle(parts[3])
-    settle(parts[4])
-    send_along_z(*GROUPS[2])
-
     @pl.when(owner)
     def _():
         others = crossed.at[0 : NZ - 1]
@@ -475,6 +471,10 @@
         def _(k):
             p = lax.rem(plane + k, 32)
             remote(final.at[chip], final.at[chip], final_s, final_r, plane_id(p)).start()
+
+    settle(parts[3])
+    settle(parts[4])
+    send_along_z(*GROUPS[2])
 
     lat_copy.wait_recv()
     half = pl.ds(pl.multiple_of(lax.rem(ctx, 2) * 8, 8), 8)

time: 41.5 us -> 42.9 us (1.034)
  the two profiles are of different devices: /device:TPU:1 before, /device:TPU:2 now
where the time goes in v7:
time: 42.9 us; the launch traced here: 42.7 us
  Pallas kernels  42.1 us (98%)
  between operations  0.64 us (1%)
    pallas_call x1, Pallas kernels, local(): pl.pallas_call(body, out_shape=(jax.ShapeDtypeStruct((1, 2, H, W, C), BF1...  41.4 us

profile of v7, /device:TPU:2, one launch (start us, length us, event | category | flops | bytes accessed | tf_op | source)
XLA Modules:
  0.0 42.7 jit_solution(14326348262714889748)
XLA Ops:
  0.6 41.4 %shard_map.155 = (bf16[1,2,8,32,256]{4,3,2,1,0:T(8,128)(2,1)S(1)}, f32[16,128]{1,0:T(8,128)S(1)}, f32[10,8,128]{2,1,0:T(8,128)S(1)}, f32[8,128]{1,0:T(8,128)S(1)}) custom-call(bf16[1,2,8,32,256]{4,3,2,1,0:T(8,128)(2,1)} %feat_hbm.1, bf16[1,2,8,32,128]{4,3,2,1,0:T(8,128)(2,1)} %grad_hbm.1, f32[1,32]{1,0:T(1,128)} %mean_hbm.1, f32[1,32]{1,0:T(1,128)} %rstd_hbm.1, ...), custom_call_target="tpu_custom_call" | custom-call | tf_op jit(solution)/shard_map/pallas_call | solution.py:553
  42.0 0.7 %shard_map.156 = (bf16[1,2,8,32,256]{4,3,2,1,0:T(8,128)(2,1)}, f32[16,108]{1,0:T(8,128)}, f32[2,16,256]{2,1,0:T(8,128)}, f32[4,256]{1,0:T(4,128)}, f32[1,1,8,16]{3,2,1,0:T(8,128)}) custom-call(bf16[1,2,8,32,256]{4,3,2,1,0:T(8,128)(2,1)S(1)} %get-tuple-element.14.fg_in, f32[16,128]{1,0:T(8,128)S(1)} %get-tuple-element.15.kg_in, ...), custom_call_target="tpu_custom_call" | custom-call | tf_op jit(solution)/shard_map/pallas_call | solution.py:626

commit v8 on v6

--- a/solution.py
+++ b/solution.py
@@ -16,7 +16,7 @@
 PX = H * W
 ROWS = 108
 TILES = 10
-PARTS = ((11, 5, "x"), (6, 3, "x"), (9, 2, "y"), (0, 3, "x"), (3, 3, "y"))
+PARTS = ((11, 5, "x"), (6, 3, "x"), (9, 2, "y"), (0, 4, "x"), (4, 2, "y"))
 GROUPS = ((11, 16), (6, 11), (0, 6))
 FAR_FIRST = (8, 7, 9, 6, 10, 5, 11, 4, 12, 3, 13, 2, 14, 1, 15)
 
@@ -382,6 +382,8 @@
 
     write_image = pltpu.make_async_copy(image, fg_ref, image_s)
     write_image.start()
+    first_stage(parts[1])
+    first_stage(parts[2])
     fields = jnp.concatenate([pools[0].reshape(2 * W, C), pools[1].reshape(2 * W, C)], axis=1)
     pooled = exact(spread, fields, ((0,), (0,)))
     normed_pool, shift_pool = pooled[:, :C], pooled[:, C:]
@@ -421,8 +423,6 @@
         def _():
             remote(small.at[t], gathered.at[plane], small_s, small_r, plane_id(tile_plane(t))).start()
 
-    first_stage(parts[1])
-    first_stage(parts[2])
     for span, term in filter_term(0, 2 * PX, 4 * PX, act[...]):
         gsum[:, span] += term
     deal(parts[3])

time: 41.5 us -> 41.8 us (level)
  no operation moved by 1% of the time
where the time goes in v8:
time: 41.8 us; the launch traced here: 41.6 us
  Pallas kernels  41 us (98%)
  between operations  0.64 us (2%)
    pallas_call x1, Pallas kernels, local(): pl.pallas_call(body, out_shape=(jax.ShapeDtypeStruct((1, 2, H, W, C), BF1...  40.3 us

profile of v8, /device:TPU:1, one launch (start us, length us, event | category | flops | bytes accessed | tf_op | source)
XLA Modules:
  0.0 41.6 jit_solution(68512040212452244)
XLA Ops:
  0.6 40.3 %shard_map.155 = (bf16[1,2,8,32,256]{4,3,2,1,0:T(8,128)(2,1)S(1)}, f32[16,128]{1,0:T(8,128)S(1)}, f32[10,8,128]{2,1,0:T(8,128)S(1)}, f32[8,128]{1,0:T(8,128)S(1)}) custom-call(bf16[1,2,8,32,256]{4,3,2,1,0:T(8,128)(2,1)} %feat_hbm.1, bf16[1,2,8,32,128]{4,3,2,1,0:T(8,128)(2,1)} %grad_hbm.1, f32[1,32]{1,0:T(1,128)} %mean_hbm.1, f32[1,32]{1,0:T(1,128)} %rstd_hbm.1, ...), custom_call_target="tpu_custom_call" | custom-call | tf_op jit(solution)/shard_map/pallas_call | solution.py:553
  40.9 0.7 %shard_map.156 = (bf16[1,2,8,32,256]{4,3,2,1,0:T(8,128)(2,1)}, f32[16,108]{1,0:T(8,128)}, f32[2,16,256]{2,1,0:T(8,128)}, f32[4,256]{1,0:T(4,128)}, f32[1,1,8,16]{3,2,1,0:T(8,128)}) custom-call(bf16[1,2,8,32,256]{4,3,2,1,0:T(8,128)(2,1)S(1)} %get-tuple-element.14.fg_in, f32[16,128]{1,0:T(8,128)S(1)} %get-tuple-element.15.kg_in, ...), custom_call_target="tpu_custom_call" | custom-call | tf_op jit(solution)/shard_map/pallas_call | solution.py:626
